TPU v7x, 32 devices: a whole 2x2x4 slice. The times are simulated.
32 devices in a mesh: groups: 2 (over y), ctx: 16 (over z, x, core).
Axes of the slice: x: 2, y: 2, z: 4, core: 2. Of those that a mesh axis runs over, the one named last changes fastest.
Arguments:
- softmax_query: bfloat16 [4096, 512], P(('groups', 'ctx')), parts along dimension 0, may hold values from -90 to 90
- softmax_key: bfloat16 [4096, 128], P(('groups', 'ctx')), parts along dimension 0, may hold values from -6 to 6
- softmax_value: bfloat16 [4096, 128], P(('groups', 'ctx')), parts along dimension 0, may hold values from -6 to 6
- softmax_output: bfloat16 [4096, 512], P(('groups', 'ctx')), parts along dimension 0, may hold values from -6 to 6
- upstream_grad: bfloat16 [4096, 512], P(('groups', 'ctx')), parts along dimension 0, may hold values from -6 to 6
- linear_query: bfloat16 [4096, 512], P(('groups', 'ctx')), parts along dimension 0, may hold values from -0.1796875 to 0.1796875
- linear_key: bfloat16 [4096, 512], P(('groups', 'ctx')), parts along dimension 0, may hold values from -0.1796875 to 0.1796875
- linear_value: bfloat16 [4096, 512], P(('groups', 'ctx')), parts along dimension 0, may hold values from -6 to 6
- linear_decay: float32 [4096, 4], P(('groups', 'ctx')), parts along dimension 0, may hold values from -1 to 0
- document_ids: int32 [4096], P('groups'), parts along dimension 0, may hold values from 0 to 3, never falling along the last dimension, each value on 1 to 1024 neighbouring positions
Outputs:
- key_gradient: bfloat16 [4096, 128], P(('groups', 'ctx')), parts along dimension 0
- value_gradient: bfloat16 [4096, 128], P(('groups', 'ctx')), parts along dimension 0
- query_cotangent: bfloat16 [4096, 512], P(('groups', 'ctx')), parts along dimension 0
- key_cotangent: bfloat16 [4096, 512], P(('groups', 'ctx')), parts along dimension 0
- value_cotangent: bfloat16 [4096, 512], P(('groups', 'ctx')), parts along dimension 0
There are 2 independent parts, one for each index of `groups`. A program takes and returns all parts, laid end to end along the dimension named above; each array names one. Nothing has to cross between parts.
All inputs are finite; a program needn't handle non-finite values.
Results may differ from a plain program's by a relative error of at most 0.0051.
Values may be sent and summed in bfloat16 or wider, within the bound.
No kernel may reach another device: no remote copies, remote signals or barrier semaphores. Data moves between devices by JAX's collectives and lax.ppermute only.
A program may use at most 256 MiB of HBM per device.

v0:
```python
import jax
import jax.numpy as jnp
from jax import lax
from jax.sharding import PartitionSpec as P

very_low = -1e30


def entering(part, axis, combine, identity, reverse):
    count = lax.axis_size(axis)
    place = lax.axis_index(axis)
    ahead = count - 1 - place if reverse else place
    gathered = jax.tree.map(lambda a: lax.all_gather(a, axis), part)
    state = jax.tree.map(lambda a, e: jnp.zeros_like(a) + jnp.asarray(e, a.dtype), part, identity)

    def one(hop, state):
        source = count - 1 - hop if reverse else hop
        return combine(
            state, jax.tree.map(lambda a: lax.dynamic_index_in_dim(a, source, 0, False), gathered)
        )

    return lax.fori_loop(0, ahead, one, state)


def chain_join(earlier, later):
    return (earlier[0] * later[0], later[1] + later[0][:, None, None] * earlier[1])


def body(
    softmax_query,
    softmax_key,
    softmax_value,
    softmax_output,
    upstream_grad,
    linear_query,
    linear_key,
    linear_value,
    linear_decay,
    document_ids,
):
    tok_rows = softmax_query.shape[0]
    head_size = softmax_key.shape[1]
    feature = softmax_query.shape[1]
    head_count = feature // head_size
    shards = lax.axis_size("ctx")
    device = lax.axis_index("ctx")
    total_rows = tok_rows * shards
    score_scaling = head_size ** (-0.5)
    highest = lax.Precision.HIGHEST
    doc_grid = document_ids.reshape(tok_rows, shards)
    query_doc = lax.dynamic_slice_in_dim(doc_grid, device, 1, 1)[:, 0]
    query_pos = jnp.arange(tok_rows, dtype=jnp.int32) * shards + device
    key_doc = doc_grid.T.reshape(total_rows)
    query_matrix = softmax_query.reshape(tok_rows, head_count, head_size)
    grads = upstream_grad.reshape(tok_rows, head_count, head_size)
    saved = softmax_output.reshape(tok_rows, head_count, head_size)
    row_delta = jnp.sum(grads.astype(jnp.float32) * saved.astype(jnp.float32), axis=-1)

    def allowed_for(offset, key_count, row_pos, row_doc):
        rows = offset + jnp.arange(key_count, dtype=jnp.int32)
        key_pos = rows % tok_rows * shards + rows // tok_rows
        docs = lax.dynamic_slice_in_dim(key_doc, offset, key_count)
        allowed = (key_pos[None, :] <= row_pos[:, None]) & (docs[None, :] == row_doc[:, None])
        return allowed[:, None, :]

    all_keys = lax.all_gather(softmax_key, "ctx", axis=0, tiled=True)
    span = tok_rows * 8

    def stat_step(carry, block_index):
        row_best, row_total = carry
        offset = block_index * span
        key_tile_block = lax.dynamic_slice_in_dim(all_keys, offset, span, 0)
        score_matrix = (
            jnp.einsum(
                "rjl,pl->rjp", query_matrix, key_tile_block, preferred_element_type=jnp.float32
            )
            * score_scaling
        )
        allowed = allowed_for(offset, span, query_pos, query_doc)
        new_best = jnp.maximum(
            row_best, jnp.max(jnp.where(allowed, score_matrix, very_low), axis=-1)
        )
        fresh = jnp.sum(
            jnp.where(allowed, jnp.exp(score_matrix - new_best[..., None]), 0.0), axis=-1
        )
        return ((new_best, row_total * jnp.exp(row_best - new_best) + fresh), None)

    start_best = jnp.full((tok_rows, head_count), very_low, jnp.float32)
    start_total = jnp.zeros((tok_rows, head_count), jnp.float32)
    (row_best, row_total), _ = lax.scan(
        stat_step, (start_best, start_total), jnp.arange(shards // 8, dtype=jnp.int32)
    )

    def tile_grads(
        query_row_set,
        gradient_rows,
        best,
        total,
        delta,
        row_pos,
        row_doc,
        key_tile_block,
        value_tile_block,
        offset,
    ):
        key_count = key_tile_block.shape[0]
        score_matrix = (
            jnp.einsum(
                "rjl,pl->rjp", query_row_set, key_tile_block, preferred_element_type=jnp.float32
            )
            * score_scaling
        )
        allowed = allowed_for(offset, key_count, row_pos, row_doc)
        weights = (
            jnp.where(allowed, jnp.exp(score_matrix - best[..., None]), 0.0) / total[..., None]
        )
        dweights = jnp.einsum(
            "rjl,pl->rjp", gradient_rows, value_tile_block, preferred_element_type=jnp.float32
        )
        score_gradient = (weights * (dweights - delta[..., None]) * score_scaling).astype(
            jnp.bfloat16
        )
        weight_reduced = weights.astype(jnp.bfloat16)
        query_part = jnp.einsum(
            "yrv,vg->yrg", score_gradient, key_tile_block, preferred_element_type=jnp.float32
        )
        key_part = jnp.einsum(
            "ghv,ghp->vp", score_gradient, query_row_set, preferred_element_type=jnp.float32
        )
        value_part = jnp.einsum(
            "ghv,ghp->vp", weight_reduced, gradient_rows, preferred_element_type=jnp.float32
        )
        return (query_part, key_part, value_part)

    def gradient_block(query_gradient, value_tile_block, offset, key_count):
        key_tile_block = lax.dynamic_slice_in_dim(all_keys, offset, key_count, 0)
        query_part, key_part, value_part = tile_grads(
            query_matrix,
            grads,
            row_best,
            row_total,
            row_delta,
            query_pos,
            query_doc,
            key_tile_block,
            value_tile_block,
            offset,
        )
        return (query_gradient + query_part, key_part, value_part)

    empty_grad = jnp.zeros((tok_rows, head_count, head_size), jnp.float32)
    value_piece = lax.all_gather(softmax_value, "ctx", axis=0, tiled=True)
    query_gradient = empty_grad
    key_count = value_piece.shape[0]
    group_size = 1
    for candidate in (2, 4, 8):
        group_size = candidate
    block_width = group_size * tok_rows
    step_count = key_count // block_width
    blocks = value_piece.reshape(step_count, block_width, head_size)

    def inner(grad_carry, item):
        block_index, value_tile_block = item
        grad_carry, key_part, value_part = gradient_block(
            grad_carry, value_tile_block, block_index * block_width, block_width
        )
        return (grad_carry, (key_part, value_part))

    query_gradient, (key_parts, value_parts) = lax.scan(
        inner, query_gradient, (jnp.arange(step_count, dtype=jnp.int32), blocks)
    )
    key_buffer = key_parts.reshape(key_count, head_size)
    value_buffer = value_parts.reshape(key_count, head_size)
    query_gradient, key_buffer, value_buffer = (query_gradient, key_buffer, value_buffer)
    key_rows, value_rows = (
        lax.psum_scatter(key_buffer, "ctx", scatter_dimension=0, tiled=True),
        lax.psum_scatter(value_buffer, "ctx", scatter_dimension=0, tiled=True),
    )
    stream = (
        (grads.astype(jnp.float32) + query_gradient).astype(jnp.bfloat16).reshape(tok_rows, feature)
    )
    per_peer = tok_rows // shards
    outbound = stream.reshape(shards, per_peer, feature).swapaxes(0, 1)
    received = lax.all_to_all(outbound, "ctx", split_axis=1, concat_axis=1, tiled=True)
    arrived = received.reshape(tok_rows, head_count, head_size)
    grad_out = arrived.astype(jnp.float32)
    lin_queries = linear_query.reshape(tok_rows, head_count, head_size).astype(jnp.float32)
    lin_keys = linear_key.reshape(tok_rows, head_count, head_size).astype(jnp.float32)
    lin_values = linear_value.reshape(tok_rows, head_count, head_size).astype(jnp.float32)
    local_doc = lax.dynamic_slice_in_dim(document_ids, device * tok_rows, tok_rows)
    prev_doc = lax.dynamic_slice_in_dim(document_ids, jnp.maximum(device * tok_rows - 1, 0), 1)[0]
    first_doc = local_doc[0]
    last_doc = local_doc[tok_rows - 1]
    link_open = ((device > 0) & (prev_doc == first_doc)).astype(jnp.float32)
    passes = (first_doc == last_doc).astype(jnp.float32)
    cumulative = jnp.cumsum(linear_decay, axis=0)
    last_cum = cumulative[tok_rows - 1]
    order = jnp.arange(tok_rows, dtype=jnp.int32)
    lower_mask = (order[:, None] >= order[None, :]) & (local_doc[:, None] == local_doc[None, :])
    cum_heads = cumulative.T
    log_ratio = cum_heads[:, :, None] - cum_heads[:, None, :]
    decay_mask = jnp.where(lower_mask[None], jnp.exp(jnp.minimum(log_ratio, 0.0)), 0.0)
    dmix = decay_mask * jnp.einsum("tav,sav->ats", grad_out, lin_values, precision=highest)
    query_cot = jnp.einsum("ats,sak->tak", dmix, lin_keys, precision=highest)
    key_cot = jnp.einsum("ats,taq->saq", dmix, lin_queries, precision=highest)
    mix = decay_mask * jnp.einsum("taq,saq->ats", lin_queries, lin_keys, precision=highest)
    value_cot = jnp.einsum("ats,tao->sao", mix, grad_out, precision=highest)
    tail_weight = (
        jnp.exp(last_cum[None, :] - cumulative)
        * (local_doc == last_doc).astype(jnp.float32)[:, None]
    )
    head_weight = (
        jnp.exp(cumulative) * (local_doc == first_doc).astype(jnp.float32)[:, None] * link_open
    )
    factor = jnp.exp(last_cum) * link_open * passes
    key_state = jnp.einsum("sa,sav,sak->avk", tail_weight, lin_values, lin_keys, precision=highest)
    grad_state = jnp.einsum(
        "ta,tao,taq->aoq", head_weight, grad_out, lin_queries, precision=highest
    )
    identity = (
        jnp.ones((head_count,), jnp.float32),
        jnp.zeros((head_count, head_size, head_size), jnp.float32),
    )
    _, earlier_state = entering((factor, key_state), "ctx", chain_join, identity, False)
    _, later_state = entering((factor, grad_state), "ctx", chain_join, identity, True)
    query_cot = query_cot + head_weight[..., None] * jnp.einsum(
        "tav,avk->tak", grad_out, earlier_state, precision=highest
    )
    key_cot = key_cot + tail_weight[..., None] * jnp.einsum(
        "sao,aoq->saq", lin_values, later_state, precision=highest
    )
    value_cot = value_cot + tail_weight[..., None] * jnp.einsum(
        "aoq,saq->sao", later_state, lin_keys, precision=highest
    )
    return (
        key_rows.astype(jnp.bfloat16),
        value_rows.astype(jnp.bfloat16),
        query_cot.reshape(tok_rows, feature).astype(jnp.bfloat16),
        key_cot.reshape(tok_rows, feature).astype(jnp.bfloat16),
        value_cot.reshape(tok_rows, feature).astype(jnp.bfloat16),
    )


def solution(mesh):
    return jax.shard_map(
        body,
        mesh=mesh,
        in_specs=(
            P(("groups", "ctx"), None),
            P(("groups", "ctx"), None),
            P(("groups", "ctx"), None),
            P(("groups", "ctx"), None),
            P(("groups", "ctx"), None),
            P(("groups", "ctx"), None),
            P(("groups", "ctx"), None),
            P(("groups", "ctx"), None),
            P(("groups", "ctx"), None),
            P("groups"),
        ),
        out_specs=(
            P(("groups", "ctx"), None),
            P(("groups", "ctx"), None),
            P(("groups", "ctx"), None),
            P(("groups", "ctx"), None),
            P(("groups", "ctx"), None),
        ),
        check_vma=False,
    )
```

profile of v0, /device:TPU:0, one launch (start us, length us, event | category | flops | bytes accessed | tf_op | source)
XLA Modules:
  0.0 326.3 jit_solution(276501529261684700)
XLA Ops:
  8.3 26.3 %all_gather.24 = bf16[2048,128]{1,0:T(8,128)(2,1)} all-gather(bf16[128,128]{1,0:T(8,128)(2,1)} %param.19), channel_id=1, replica_groups=mesh['groups'=2,'ctx'=16] {'ctx'}, dimensions={0}, use_global_device_ids=true | all-gather | bytes 557056 | tf_op jit(solution)/shard_map/all_gather | solution.py:66
  35.8 7.1 %while.60 = (s32[]{:T(128)}, f32[128,4]{0,1:T(4,128)S(1)}, f32[128,4]{0,1:T(4,128)S(1)}, s32[2]{0:T(128)S(1)}, s32[2048]{0:T(1024)S(1)}, /*index=5*/s32[128,1]{0...) while((s32[]{:T(128)}, f32[128,4]{0,1:T(4,128)S(1)}, ...), condition=%wide.region_3.4_spmd.clone, body=%wide.region_0.3_spmd.clone.sunk | while | flops 138306304 | bytes 5029594 | solution.py:90
  37.5 1.4 fusion.124
  41.0 1.4 fusion.124
  42.9 20.3 %all_gather.25 = bf16[2048,128]{1,0:T(8,128)(2,1)} all-gather(bf16[128,128]{1,0:T(8,128)(2,1)S(1)} %copy-done.15), channel_id=1, replica_groups=mesh['groups'=2,'ctx'=16] {'ctx'}, dimensions={0}, use_global_device_ids=true | all-gather | bytes 557056 | tf_op jit(solution)/shard_map/all_gather | solution.py:152
  64.0 17.6 %while.61 = (s32[]{:T(128)}, f32[128,4,128]{2,0,1:T(8,128)}, f32[2,1024,128]{2,1,0:T(8,128)}, f32[2,1024,128]{2,1,0:T(8,128)}, s32[2]{0:T(128)S(1)}, /*index=5*/...) while((s32[]{:T(128)}, f32[128,4,128]{2,0,1:T(8,128)}, ...), condition=%wide.region_6.7_spmd.clone, body=%wide.region_5.6_spmd.clone.sunk | while | flops 676354304 | bytes 23117908 | solution.py:169
  65.7 1.6 fusion.138
  67.8 2.2 convolution_add_fusion.2
  70.0 1.3 fusion.140
  74.4 1.6 fusion.138
  76.6 2.3 convolution_add_fusion.2
  78.9 1.2 fusion.140
  83.5 1.3 dynamic_slice.81
  88.1 2.1 compare_convert_fusion.1
  92.4 3.5 %all-to-all-start = ((bf16[8,16,512]{2,0,1:T(8,128)(2,1)}), bf16[8,16,512]{2,0,1:T(8,128)(2,1)S(1)}, u32[]{:S(2)}, u32[]{:S(2)}) async-start(bf16[8,16,512]{2,0,1:T(8,128)(2,1)} %bitcast.13), calls=%async_computation.2 | async-start | bytes 262144 | tf_op jit(solution)/shard_map/all_to_all | solution.py:184
  96.1 7.8 %all-to-all-done = bf16[8,16,512]{2,0,1:T(8,128)(2,1)S(1)} async-done(((bf16[8,16,512]{2,0,1:T(8,128)(2,1)}), bf16[8,16,512]{2,0,1:T(8,128)(2,1)S(1)}, u32[]{:S(2)}, u32[]{:S(2)}) %all-to-all-start) | async-done | bytes 131104 | tf_op jit(solution)/shard_map/all_to_all | solution.py:184
  105.1 18.1 %all-gather.2 = f32[16,1,4]{2,1,0:T(1,128)S(1)} all-gather(f32[1,1,4]{2,1,0:T(1,128)S(1)} %get-tuple-element.735), channel_id=1, replica_groups=mesh['groups'=2,'ctx'=16] {'ctx'}, dimensions={0}, use_global_device_ids=true | all-gather | bytes 272 | tf_op jit(solution)/shard_map/all_gather | solution.py:13
  125.0 13.0 %reduce-scatter.3.cloned.1.call-done = f32[128,128]{1,0:T(8,128)} async-done(((f32[2048,128]{1,0:T(8,128)}), f32[128,128]{1,0:T(8,128)}) %reduce-scatter.3.cloned.1.call-update) | async-done | bytes 65552 | tf_op jit(solution)/shard_map/reduce_scatter | solution.py:176
  138.0 1.5 convert_element_type.68
  139.4 58.8 %reduce-scatter.5.cloned.1.call-done = f32[128,128]{1,0:T(8,128)} async-done(((f32[2048,128]{1,0:T(8,128)}), f32[128,128]{1,0:T(8,128)}) %reduce-scatter.5.cloned.1.call-update) | async-done | bytes 65552 | tf_op jit(solution)/shard_map/reduce_scatter | solution.py:177
  198.3 1.5 convert_element_type.69
  199.7 50.2 %all-gather.6.cloned.1.call-done = f32[64,128,128]{2,1,0:T(8,128)} async-done(((f32[4,128,128]{2,1,0:T(8,128)}), f32[64,128,128]{2,1,0:T(8,128)}) %all-gather.6.cloned.1.call-update) | async-done | bytes 4194320 | tf_op jit(solution)/shard_map/all_gather | solution.py:13
  251.1 49.8 %all-gather.8.cloned.1.call-done = f32[64,128,128]{2,1,0:T(8,128)} async-done(((f32[4,128,128]{2,1,0:T(8,128)}), f32[64,128,128]{2,1,0:T(8,128)}) %all-gather.8.cloned.1.call-update) | async-done | bytes 4194320 | tf_op jit(solution)/shard_map/all_gather | solution.py:13
  300.9 16.5 %while.59 = (s32[]{:T(128)}, f32[4,128,128]{2,1,0:T(8,128)S(1)}, s32[]{:T(128)}, f32[16,4,128,128]{3,2,1,0:T(8,128)}, f32[16,4]{1,0:T(8,128)S(1)}, /*index=5*/s32[]{:T(128)}, s32[]{:T(128)}, s32[]{:T(128)}, s32[]{:T(128)}) while((s32[]{:T(128)}, f32[4,128,128]{2,1,0:T(8,128)S(1)}, s32[]{:T(128)}, f32[16,4,128,128]{3,2,1,0:T(8,128)}, ...), condition=%wide.region_13.14_spmd, body=%wide.region_12.13_spmd.sunk | while | flops 131078 | bytes 786635 | solution.py:22
  (179 shorter events, 39.0 us)
Async XLA Ops:
  7.2 83.2 %copy-start = (bf16[128,512]{1,0:T(8,128)(2,1)S(1)}, bf16[128,512]{1,0:T(8,128)(2,1)}, u32[]{:S(2)}) copy-start(bf16[128,512]{1,0:T(8,128)(2,1)} %param.24) | copy-start | bytes 393220
  7.2 130.8 %reduce-scatter.3.cloned.1.call-start = ((), (), s32[]{:S(2)}) async-start(), calls=%async_computation.3 | async-start | bytes 1114112 | tf_op jit(solution)/shard_map/reduce_scatter | solution.py:176
  35.8 7.2 %copy-start.15 = (bf16[128,128]{1,0:T(8,128)(2,1)S(1)}, bf16[128,128]{1,0:T(8,128)(2,1)}, u32[]{:S(2)}) copy-start(bf16[128,128]{1,0:T(8,128)(2,1)} %param.20) | copy-start | bytes 98308
  35.8 27.4 %copy-start.8 = (bf16[128,512]{1,0:T(8,128)(2,1)S(1)}, bf16[128,512]{1,0:T(8,128)(2,1)}, u32[]{:S(2)}) copy-start(bf16[128,512]{1,0:T(8,128)(2,1)} %param.22) | copy-start | bytes 393220
  35.8 27.7 %copy-start.9 = (bf16[128,512]{1,0:T(8,128)(2,1)S(1)}, bf16[128,512]{1,0:T(8,128)(2,1)}, u32[]{:S(2)}) copy-start(bf16[128,512]{1,0:T(8,128)(2,1)} %param.21) | copy-start | bytes 393220
  64.0 3.3 %copy-start.11 = (s32[128,1]{0,1:T(1,128)}, s32[128,1]{0,1:T(1,128)S(1)}, u32[]{:S(2)}) copy-start(s32[128,1]{0,1:T(1,128)S(1)} %get-tuple-element.1038) | copy-start | bytes 1540 | tf_op jit(solution)/shard_map/while
  64.0 3.3 %copy-start.13 = (f32[128,4]{0,1:T(4,128)}, f32[128,4]{0,1:T(4,128)S(1)}, u32[]{:S(2)}) copy-start(f32[128,4]{0,1:T(4,128)S(1)} %get-tuple-element.1042) | copy-start | bytes 6148 | tf_op jit(solution)/shard_map/while
  64.0 3.3 %copy-start.17 = (s32[2]{0:T(128)}, s32[2]{0:T(128)S(1)}, u32[]{:S(2)}) copy-start(s32[2]{0:T(128)S(1)} %get-tuple-element.1036) | copy-start | bytes 28 | tf_op jit(solution)/shard_map/while
  65.6 1.7 copy-start.2
  67.8 3.5 %copy-start.5 = (f32[2,1024,128]{2,1,0:T(8,128)S(1)}, f32[2,1024,128]{2,1,0:T(8,128)}, u32[]{:S(2)}) copy-start(f32[2,1024,128]{2,1,0:T(8,128)} %get-tuple-element.1016) | copy-start | bytes 3145732 | tf_op jit(solution)/shard_map/while
  71.3 1.4 copy-start.14
  71.3 1.4 copy-start.18
  72.8 3.3 %copy-start.11 = (s32[128,1]{0,1:T(1,128)}, s32[128,1]{0,1:T(1,128)S(1)}, u32[]{:S(2)}) copy-start(s32[128,1]{0,1:T(1,128)S(1)} %get-tuple-element.1038) | copy-start | bytes 1540 | tf_op jit(solution)/shard_map/while
  72.8 3.3 %copy-start.13 = (f32[128,4]{0,1:T(4,128)}, f32[128,4]{0,1:T(4,128)S(1)}, u32[]{:S(2)}) copy-start(f32[128,4]{0,1:T(4,128)S(1)} %get-tuple-element.1042) | copy-start | bytes 6148 | tf_op jit(solution)/shard_map/while
  72.8 3.3 %copy-start.17 = (s32[2]{0:T(128)}, s32[2]{0:T(128)S(1)}, u32[]{:S(2)}) copy-start(s32[2]{0:T(128)S(1)} %get-tuple-element.1036) | copy-start | bytes 28 | tf_op jit(solution)/shard_map/while
  74.4 1.7 copy-start.2
  76.6 3.5 %copy-start.5 = (f32[2,1024,128]{2,1,0:T(8,128)S(1)}, f32[2,1024,128]{2,1,0:T(8,128)}, u32[]{:S(2)}) copy-start(f32[2,1024,128]{2,1,0:T(8,128)} %get-tuple-element.1016) | copy-start | bytes 3145732 | tf_op jit(solution)/shard_map/while
  81.6 9.8 %copy-start.1 = (f32[128,4,128]{2,0,1:T(8,128)S(1)}, f32[128,4,128]{2,0,1:T(8,128)}, u32[]{:S(2)}) copy-start(f32[128,4,128]{2,0,1:T(8,128)} %get-tuple-element.444) | copy-start | bytes 786436
  81.6 9.9 %copy-start.4 = (bf16[128,512]{0,1:T(8,128)(2,1)S(1)}, bf16[128,512]{0,1:T(8,128)(2,1)}, u32[]{:S(2)}) copy-start(bf16[128,512]{0,1:T(8,128)(2,1)} %copy-done.3) | copy-start | bytes 393220
  81.6 116.6 %reduce-scatter.5.cloned.1.call-start = ((), (), s32[]{:S(2)}) async-start(), calls=%async_computation.4 | async-start | bytes 1114112 | tf_op jit(solution)/shard_map/reduce_scatter | solution.py:177
  82.4 167.5 %all-gather.6.cloned.1.call-start = ((), (), s32[]{:S(2)}) async-start(), calls=%async_computation.5 | async-start | bytes 4456448 | tf_op jit(solution)/shard_map/all_gather | solution.py:13
  82.5 21.6 %copy-start.7 = (bf16[128,512]{1,0:T(8,128)(2,1)S(1)}, bf16[128,512]{1,0:T(8,128)(2,1)}, u32[]{:S(2)}) copy-start(bf16[128,512]{1,0:T(8,128)(2,1)} %param.23) | copy-start | bytes 393220
  92.4 11.4 %all-to-all-start = ((bf16[8,16,512]{2,0,1:T(8,128)(2,1)}), bf16[8,16,512]{2,0,1:T(8,128)(2,1)S(1)}, u32[]{:S(2)}, u32[]{:S(2)}) async-start(bf16[8,16,512]{2,0,1:T(8,128)(2,1)} %bitcast.13), calls=%async_computation.2 | async-start | bytes 262144 | tf_op jit(solution)/shard_map/all_to_all | solution.py:184
  95.9 205.0 %all-gather.8.cloned.1.call-start = ((), (), s32[]{:S(2)}) async-start(), calls=%async_computation.6 | async-start | bytes 4456448 | tf_op jit(solution)/shard_map/all_gather | solution.py:13
  (9 other events, 10.4 us)
Sparse Core Ops, SparseCore 0:
  81.8 56.1 reduce-scatter.2
  141.6 56.6 reduce-scatter.4
  200.4 49.4 all-gather.5
  251.9 48.9 all-gather.7
where the time goes:
time: 327 us; the launch traced here: 326 us
  waiting for transfers between devices  180 us (55%)
  blocking collectives  64.7 us (20%)
  other arithmetic  23.7 us (7%)
  matrix products  19.4 us (6%)
  between operations  16.7 us (5%)
  local copies, waits for them, and re-layouts  14.2 us (4%)
  starting transfers between devices  3.68 us (1%)
  loops' own time  3.48 us (1%)
    all_gather x2, waiting for transfers between devices, entering(): gathered = jax.tree.map(lambda a: lax.all_gather(a, axis), part)  100 us
    reduce_scatter x1, waiting for transfers between devices, body(): lax.psum_scatter(value_buffer, 'ctx', scatter_dimension=0, tiled=True)  58.8 us
    all_gather x1, blocking collectives, body(): all_keys = lax.all_gather(softmax_key, 'ctx', axis=0, tiled=True)  26.3 us
    all_gather x1, blocking collectives, body(): value_piece = lax.all_gather(softmax_value, 'ctx', axis=0, tiled=True)  20.3 us
    all_gather x1, blocking collectives, entering(): gathered = jax.tree.map(lambda a: lax.all_gather(a, axis), part)  18.1 us
    add x15, other arithmetic, chain_join(): later[1] + later[0][:, None, None] * earlier[1]  15.9 us
    reduce_scatter x1, waiting for transfers between devices, body(): lax.psum_scatter(key_buffer, 'ctx', scatter_dimension=0, tiled=True)  13 us
    all_to_all x1, waiting for transfers between devices, body(): lax.all_to_all(outbound, 'ctx', split_axis=1, concat_axis=1, tiled=True)  7.76 us
  transfers between devices with their start and end apart: 5, of which 5 were waited for; matrix products, arithmetic and copies ran while one was open for 4% of the time, Pallas kernels for 0%

commit v1 on v0

v1 whole, which is shorter than its diff:
```python
import functools

import jax
import jax.numpy as jnp
from jax import lax
from jax.experimental import pallas as pl
from jax.experimental.pallas import tpu as pltpu
from jax.sharding import Mesh
from jax.sharding import PartitionSpec as P

very_low = -1e30
f32, bf16, i32 = jnp.float32, jnp.bfloat16, jnp.int32
DEC_ROWS = 16
VMEM = pl.BlockSpec(memory_space=pltpu.VMEM)
SMEM = pl.BlockSpec(memory_space=pltpu.SMEM)


def nt(a, b):
    return lax.dot_general(a, b, (((1,), (1,)), ((), ())), preferred_element_type=f32)


def nn(a, b):
    return lax.dot_general(a, b, (((1,), (0,)), ((), ())), preferred_element_type=f32)


def tn(a, b):
    return lax.dot_general(a, b, (((0,), (0,)), ((), ())), preferred_element_type=f32)


def iota(shape, dim):
    return lax.broadcasted_iota(i32, shape, dim)


def quot(x, d):
    return ((x.astype(f32) + 0.5) * (1.0 / d)).astype(i32)


def run_starts(docs):
    counts = []
    for v in (1, 2, 3):
        hit = jnp.where(docs < v, 1.0, 0.0)
        total = jnp.sum(jnp.sum(hit, axis=0, keepdims=True), axis=1, keepdims=True)
        counts.append(total.astype(i32))
    return counts


def start_of(pos, bounds):
    start = jnp.zeros_like(pos)
    for b in bounds:
        start = jnp.maximum(start, jnp.where(pos >= b, b, 0))
    return start


def chunks(count, body):
    if count <= 8:
        for i in range(count):
            body(i)
    else:
        lax.fori_loop(0, count, lambda i, c: (body(i), c)[1], 0)


def at(i, size):
    return pl.ds(i * size if isinstance(i, int) else pl.multiple_of(i * size, size), size)


def sums(dec_row):
    span = dec_row.shape[1]
    col, row = iota((span, span), 0), iota((span, span), 1)
    c_col = jnp.sum(jnp.where(row <= col, dec_row, 0.0), axis=1, keepdims=True)
    c_row = jnp.sum(jnp.where(row == col, c_col, 0.0), axis=0, keepdims=True)
    return c_row, c_col


def pack_linear(heads, idx_ref, q_ref, k_ref, v_ref, dec_ref, *rest):
    outs, scr = rest[:heads], rest[heads]
    tok, head = q_ref.shape[0], q_ref.shape[1] // heads
    p = lax.rem(idx_ref[0], heads)
    scr[...] = jnp.concatenate([dec_ref[...], jnp.zeros((tok, head - heads), f32)], axis=1).T
    for k in range(heads):
        h = p ^ k
        lanes = pl.ds(pl.multiple_of(h * head, head), head)
        out = outs[k]
        out[0:tok, :] = q_ref[:, lanes]
        out[tok : 2 * tok, :] = k_ref[:, lanes]
        out[2 * tok : 3 * tok, :] = v_ref[:, lanes]
        d = scr[pl.ds(h, 1), :]
        hi = d.astype(bf16)
        left = d - hi.astype(f32)
        mid = left.astype(bf16)
        low = (left - mid.astype(f32)).astype(bf16)
        r = iota((DEC_ROWS, head), 0)
        rows = jnp.where(r == 0, hi.astype(f32), jnp.where(r == 1, mid.astype(f32), jnp.where(r == 2, low.astype(f32), 0.0)))
        out[3 * tok : 3 * tok + DEC_ROWS, :] = rows.astype(bf16)


def pack_main(heads, planes, window, idx_ref, q_ref, k_ref, v_ref, o_ref, g_ref, out):
    tok, head = k_ref.shape
    rp, xs = tok // planes, heads // 2
    zx = lax.div(idx_ref[0], 2)
    wide = xs * planes * rp
    cols = []
    for a in range(heads):
        s = slice(a * head, (a + 1) * head)
        cols.append(jnp.sum(g_ref[:, s].astype(f32) * o_ref[:, s].astype(f32), axis=1, keepdims=True))
    r, lane = iota((tok, wide), 0), iota((tok, wide), 1) - zx * rp
    r8 = iota((8, wide), 0)
    for g in range(planes):
        hit = (lane == r - g * rp) & (lane >= 0) & (lane < rp)
        rows = [jnp.sum(jnp.where(hit, c, 0.0), axis=0, keepdims=True) for c in cols]
        for x in range(xs):
            to = g * xs + x
            s = slice(x * 2 * head, (x + 1) * 2 * head)
            out[to, 0:rp, :] = q_ref[g * rp : (g + 1) * rp, s]
            out[to, rp : 2 * rp, :] = g_ref[g * rp : (g + 1) * rp, s]
            for w in range(window):
                plane = (g - window + 1 + w) % planes
                rows_w = slice((2 + w) * rp, (3 + w) * rp)
                out[to, rows_w, 0:head] = k_ref[plane * rp : (plane + 1) * rp, :]
                out[to, rows_w, head : 2 * head] = v_ref[plane * rp : (plane + 1) * rp, :]
            d0, d1 = rows[2 * x], rows[2 * x + 1]
            h0, h1 = d0.astype(bf16).astype(f32), d1.astype(bf16).astype(f32)
            tail = jnp.where(r8 == 0, h0, jnp.where(r8 == 1, d0 - h0, jnp.where(r8 == 2, h1, jnp.where(r8 == 3, d1 - h1, 0.0))))
            out[to, (2 + window) * rp : (2 + window) * rp + 8, :] = tail.astype(bf16)


def pack_main_plain(heads, planes, window, idx, q, k, v, o, grad):
    tok, head = k.shape
    rp, xs = tok // planes, heads // 2
    zx = idx[0] // 2
    wide = xs * planes * rp

    def pieces(a):
        return a.reshape(planes, rp, xs, 2 * head).swapaxes(1, 2).reshape(planes * xs, rp, 2 * head)

    kv = jnp.concatenate([k, v], axis=1).reshape(planes, rp, 2 * head)
    win = jnp.stack([jnp.roll(kv, window - 1 - w, axis=0) for w in range(window)], axis=1)
    win = jnp.repeat(win.reshape(planes, 1, window * rp, 2 * head), xs, axis=1)
    win = win.reshape(planes * xs, window * rp, 2 * head)
    delta = jnp.sum((grad.astype(f32) * o.astype(f32)).reshape(tok, heads, head), axis=-1)
    high = lax.reduce_precision(delta, 8, 7)
    parts = jnp.stack([high, delta - high], axis=-1).astype(bf16)
    parts = parts.reshape(planes, rp, xs, 4).transpose(0, 2, 3, 1).reshape(planes * xs, 4, rp)
    tail = jnp.zeros((planes * xs, 8, wide), bf16)
    tail = lax.dynamic_update_slice(tail, parts, (0, 0, zx * rp))
    return jnp.concatenate([pieces(q), pieces(grad), win, tail], axis=1)


def gather_linear(heads, idx_ref, docs_ref, *rest):
    msgs, (qkv, dec, state) = rest[:heads], rest[heads:]
    tok, head = (msgs[0].shape[0] - DEC_ROWS) // 3, msgs[0].shape[1]
    p, g = lax.rem(idx_ref[0], heads), lax.div(idx_ref[0], heads)
    span = heads * tok
    for k in range(heads):
        off = pl.multiple_of((p ^ k) * tok, tok)
        for j in range(3):
            qkv[j, pl.ds(off, tok), :] = msgs[k][j * tok : (j + 1) * tok, :]
        parts = msgs[k][3 * tok : 3 * tok + DEC_ROWS, :].astype(f32)
        dec[:, pl.ds(off, tok)] = jnp.broadcast_to(jnp.sum(parts, axis=0, keepdims=True), (8, tok))
    bounds = run_starts(docs_ref[...])
    dec_row = dec[0:1, :]
    _, c_col = sums(dec_row)
    total = jnp.sum(dec_row, axis=1, keepdims=True)
    pos = g * span + iota((span, 1), 0)
    last = start_of(jnp.zeros((1, 1), i32) + (g * span + span - 1), bounds)
    tail = jnp.where(pos >= last, jnp.exp(jnp.minimum(total - c_col, 0.0)), 0.0)
    weighted = (qkv[2].astype(f32) * tail).astype(bf16)
    state[0:head, :] = tn(weighted, qkv[1])
    state[head : head + 8, :] = jnp.broadcast_to(total, (8, head))


def softmax_kernel(cfg, *refs):
    heads, planes, window, tok, aligned = cfg
    if aligned:
        idx_ref, docs_ref, own, other, qkv, dec, keep, give, stream_out, state, s_scr, p_scr, ds_scr = refs
    else:
        idx_ref, docs_ref, q_in, g_in, kv_in, delta_in, qkv, dec, keep, give, stream_out, state, s_scr, p_scr, ds_scr = refs
    head = keep.shape[1] // 2
    rp, owners = tok // planes, heads * planes // 2
    n = 2 * owners
    half_keys = owners * window * rp
    keys, span = 2 * half_keys, heads * tok
    scale = head ** (-0.5)
    me = idx_ref[0]
    core, g = lax.rem(me, 2), lax.div(me, heads)
    bounds = run_starts(docs_ref[...])

    if aligned:
        mine = pl.ds(pl.multiple_of(core * head, head), head)
        kv_rows = slice(2 * rp, (2 + window) * rp)

        def both(rows, lanes):
            count = owners * (rows.stop - rows.start)
            return jnp.concatenate([ref[:, rows, lanes].reshape(count, head) for ref in (own, other)], axis=0)

        q = both(slice(0, rp), mine)
        grad = both(slice(rp, 2 * rp), mine)
        key = both(kv_rows, slice(0, head))
        value = both(kv_rows, slice(head, 2 * head))
        tails = []
        for ref in (own, other):
            t = jnp.zeros((8, owners * rp), f32)
            for o in range(owners):
                t = t + ref[o, (2 + window) * rp : (2 + window) * rp + 8, :].astype(f32)
            tails.append(jnp.where(core == 0, t[0:1] + t[1:2], t[2:3] + t[3:4]))
        delta = jnp.concatenate(tails, axis=1)
    else:
        q, grad = q_in[...], g_in[...]
        key, value = kv_in[:, 0:head], kv_in[:, head : 2 * head]
        delta = delta_in[0:1, :]

    j = iota((1, span), 1)
    side = quot(j, owners * rp)
    inner = j - side * (owners * rp)
    zx = quot(inner, rp)
    q_rel = (inner - zx * rp) * n + zx * 2 + jnp.where(side == 0, core, 1 - core)
    q_pos = q_rel + g * span
    q_start = start_of(q_pos, bounds)

    def key_pos(first, count):
        j = iota((count, 1), 0) + first
        side = jnp.where(j >= half_keys, 1, 0)
        inner = j - side * half_keys
        zx = quot(inner, window * rp)
        row = inner - zx * (window * rp) + (g - window + 1) * rp
        row = jnp.where(row < 0, row + tok, row)
        return row * n + zx * 2 + jnp.where(side == 0, core, 1 - core)

    if aligned:
        wide, deep = 256, 256
    else:
        wide, deep = 128, 256
    steps = keys // deep
    for b in range(span // wide):
        lanes = slice(b * wide, (b + 1) * wide)
        qb, gb = q[lanes, :], grad[lanes, :]
        lo, hi, db = q_start[:, lanes], q_pos[:, lanes], delta[:, lanes]

        def first(i, best):
            rows = at(i, deep)
            kc = key[i * deep : (i + 1) * deep] if aligned else kv_in[rows, 0:head]
            s = nt(kc, qb)
            pos = key_pos(i * deep, deep)
            s = jnp.where((pos >= lo) & (pos <= hi), s, very_low)
            s_scr[rows, :] = s
            return jnp.maximum(best, jnp.max(s.reshape(deep // 8, 8, wide), axis=0))

        def second(i, acc):
            rows = at(i, deep)
            e = jnp.exp((s_scr[rows, :] - best) * scale)
            s_scr[rows, :] = e
            return acc + jnp.sum(e.reshape(deep // 8, 8, wide), axis=0)

        def third(i):
            rows = at(i, deep)
            vc = value[i * deep : (i + 1) * deep] if aligned else kv_in[rows, head : 2 * head]
            pr = s_scr[rows, :] * inv
            dp = nt(vc, gb)
            p_scr[rows, lanes] = pr.astype(bf16)
            ds_scr[rows, lanes] = (pr * (dp - db) * scale).astype(bf16)

        best = jnp.full((8, wide), very_low, f32)
        acc = jnp.zeros((8, wide), f32)
        if aligned:
            for i in range(steps):
                best = first(i, best)
            best = jnp.max(best, axis=0, keepdims=True)
            for i in range(steps):
                acc = second(i, acc)
            inv = 1.0 / jnp.sum(acc, axis=0, keepdims=True)
            for i in range(steps):
                third(i)
        else:
            best = jnp.max(lax.fori_loop(0, steps, first, best), axis=0, keepdims=True)
            inv = 1.0 / jnp.sum(lax.fori_loop(0, steps, second, acc), axis=0, keepdims=True)
            lax.fori_loop(0, steps, lambda i, c: (third(i), c)[1], 0)

    eye = jnp.where(iota((head, head), 0) == iota((head, head), 1), 1.0, 0.0).astype(bf16)
    dq_t = tn(key, ds_scr[...])
    stream_t = (nt(eye, grad) + dq_t).astype(bf16)
    order = jnp.where(iota((span, span), 0) == q_rel, 1.0, 0.0).astype(bf16)
    stream = nt(order, stream_t).astype(bf16)
    stream_out[...] = stream

    _, c_col = sums(dec[0:1, :])
    start = start_of(iota((span, 1), 0) + g * span, bounds)
    weight = jnp.where(start < g * span, jnp.exp(c_col), 0.0)
    state[0:head, :] = tn((stream.astype(f32) * weight).astype(bf16), qkv[0])
    state[head : head + 8, :] = jnp.broadcast_to(jnp.sum(dec[0:1, :], axis=1, keepdims=True), (8, head))

    for i, out in enumerate((keep, give)):
        rows = slice(i * half_keys, (i + 1) * half_keys)
        out[:, 0:head] = nn(ds_scr[rows, :], q).astype(out.dtype)
        out[:, head : 2 * head] = nn(p_scr[rows, :], grad).astype(out.dtype)


def joined(states, g, span, bounds, step):
    head = states[0].shape[1]
    one = jnp.zeros((1, 1), i32)
    total, passed = None, jnp.zeros((1, 1), f32)
    for k, ref in enumerate(states, 1):
        if step < 0:
            open_ = start_of(one + (g * span - 1), bounds) < (g - k + 1) * span
        else:
            open_ = start_of(one + ((g + k) * span - 1), bounds) < (g + 1) * span
        part = ref[0:head, :] * jnp.where(open_, jnp.exp(passed), 0.0)
        total = part if total is None else total + part
        passed = passed + ref[head : head + 1, 0:1]
    return total


def linear_kernel(heads, idx_ref, docs_ref, stream_ref, qkv, dec, *rest):
    states, (q_out, k_out, v_out, dm, mx) = rest[:-5], rest[-5:]
    span, head = stream_ref.shape
    g = lax.div(idx_ref[0], heads)
    bounds = run_starts(docs_ref[...])
    earlier = joined(states, g, span, bounds, -1)
    c_row, c_col = sums(dec[0:1, :])
    stream, query, key, value = stream_ref[...], qkv[0], qkv[1], qkv[2]
    t = iota((1, span), 1)
    lo = start_of(t + g * span, bounds) - g * span
    deep = 128
    for i in range(span // deep):
        rows = slice(i * deep, (i + 1) * deep)
        s = iota((deep, 1), 0) + i * deep
        ratio = jnp.minimum(c_row - c_col[rows], 0.0)
        decay = jnp.where((s <= t) & (s >= lo), jnp.exp(ratio), 0.0)
        dm[rows, :] = (decay * nt(value[rows], stream)).astype(bf16)
        mx[rows, :] = (decay * nt(key[rows], query)).astype(bf16)
    start = start_of(iota((span, 1), 0) + g * span, bounds)
    weight = jnp.where(start < g * span, jnp.exp(c_col), 0.0)
    q_out[...] = (tn(dm[...], key) + weight * nn(stream, earlier.astype(bf16))).astype(bf16)
    k_out[...] = nn(dm[...], query)
    v_out[...] = nn(mx[...], stream)


def finish_kernel(heads, idx_ref, docs_ref, q_ref, k_ref, v_ref, qkv, dec, *rest):
    states, outs, (k_scr, v_scr) = rest[: -2 - heads], rest[-2 - heads : -2], rest[-2:]
    span, head = q_ref.shape
    tok = span // heads
    p, g = lax.rem(idx_ref[0], heads), lax.div(idx_ref[0], heads)
    bounds = run_starts(docs_ref[...])
    later = joined(states, g, span, bounds, 1).astype(bf16)
    _, c_col = sums(dec[0:1, :])
    total = jnp.sum(dec[0:1, :], axis=1, keepdims=True)
    pos = g * span + iota((span, 1), 0)
    last = start_of(jnp.zeros((1, 1), i32) + (g * span + span - 1), bounds)
    tail = jnp.where(pos >= last, jnp.exp(jnp.minimum(total - c_col, 0.0)), 0.0)
    k_scr[...] = (k_ref[...] + tail * nn(qkv[2], later)).astype(bf16)
    v_scr[...] = (v_ref[...] + tail * nt(qkv[1], later)).astype(bf16)
    for k in range(heads):
        rows = pl.ds(pl.multiple_of((p ^ k) * tok, tok), tok)
        outs[k][0:tok, :] = q_ref[rows, :]
        outs[k][tok : 2 * tok, :] = k_scr[rows, :]
        outs[k][2 * tok : 3 * tok, :] = v_scr[rows, :]


def spread_kernel(heads, idx_ref, *rest):
    msgs, outs = rest[:heads], rest[heads:]
    tok, head = outs[0].shape[0], outs[0].shape[1] // heads
    p = lax.rem(idx_ref[0], heads)
    for k in range(heads):
        lanes = pl.ds(pl.multiple_of((p ^ k) * head, head), head)
        for j in range(3):
            outs[j][:, lanes] = msgs[k][j * tok : (j + 1) * tok, :]


def total_kernel(planes, xs, window, parts, k_out, v_out):
    tok, head = k_out.shape
    rp = tok // planes
    for q in range(planes):
        total = None
        for j in range(window):
            w = window - 1 - j
            for x in range(xs):
                part = parts[((q + j) % planes) * xs + x, w * rp : (w + 1) * rp, :].astype(f32)
                total = part if total is None else total + part
        rows = slice(q * rp, (q + 1) * rp)
        k_out[rows, :] = total[:, 0:head].astype(bf16)
        v_out[rows, :] = total[:, head : 2 * head].astype(bf16)


def call(body, ins, outs, scratch=(), flops=1 << 20):
    in_specs = [SMEM if a.dtype == i32 and a.ndim == 1 else VMEM for a in ins]
    return pl.pallas_call(
        body,
        in_specs=in_specs,
        out_specs=tuple(VMEM for _ in outs),
        out_shape=tuple(jax.ShapeDtypeStruct(*o) for o in outs),
        scratch_shapes=list(scratch),
        compiler_params=pltpu.CompilerParams(vmem_limit_bytes=60000 * 1024),
        cost_estimate=pl.CostEstimate(flops=flops, bytes_accessed=1 << 20, transcendentals=0),
    )(*ins)


def body(
    softmax_query,
    softmax_key,
    softmax_value,
    softmax_output,
    upstream_grad,
    linear_query,
    linear_key,
    linear_value,
    linear_decay,
    document_ids,
):
    tok, head = softmax_key.shape
    heads = softmax_query.shape[1] // head
    n = lax.axis_size("zx") * lax.axis_size("core")
    planes, xs = n // heads, heads // 2
    rp = tok // planes
    window = min(planes, planes // 2 + 1)
    owners = n // 2
    span = heads * tok
    half_keys = owners * window * rp
    aligned = rp % 16 == 0
    me = (lax.axis_index("zx") * 2 + lax.axis_index("core")).astype(i32)
    idx = me.reshape(1)
    docs = document_ids.reshape(-1, 128)
    line = ("zx", "core")

    def swap(a, k):
        return lax.ppermute(a, line, [(i, i ^ k) for i in range(n)])

    def shift(a, k):
        pairs = [(i, i + k * heads) for i in range(n) if 0 <= i + k * heads < n]
        return lax.ppermute(a, line, pairs)

    msg = ((3 * tok + DEC_ROWS, head), bf16)
    lin = call(
        functools.partial(pack_linear, heads),
        (idx, linear_query, linear_key, linear_value, linear_decay),
        (msg,) * heads,
        [pltpu.VMEM((head, tok), f32)],
    )
    lin = [lin[0]] + [swap(lin[k], k) for k in range(1, heads)]

    packed = (idx, softmax_query, softmax_key, softmax_value, softmax_output, upstream_grad)
    if aligned:
        rows = (2 + window) * rp + 8
        send = call(
            functools.partial(pack_main, heads, planes, window), packed, (((owners, rows, 2 * head), bf16),)
        )[0]
    else:
        send = pack_main_plain(heads, planes, window, *packed)
    own = lax.all_to_all(send, "zx", 0, 0, tiled=True)
    other = swap(own, 1)

    state = ((head + 8, head), f32)
    qkv, dec, forward = call(
        functools.partial(gather_linear, heads),
        (idx, docs, *lin),
        (((3, span, head), bf16), ((8, span), f32), state),
    )
    before = [shift(forward, k) for k in range(1, window)]

    if aligned:
        given = (own, other)
        wide = 256
    else:
        core = me % 2
        halves = [lax.dynamic_slice_in_dim(a, core * head, head, 2) for a in (own, other)]
        q = jnp.concatenate([a[:, 0:rp].reshape(owners * rp, head) for a in halves])
        grad = jnp.concatenate([a[:, rp : 2 * rp].reshape(owners * rp, head) for a in halves])
        kv = jnp.concatenate([a[:, 2 * rp : -8].reshape(half_keys, 2 * head) for a in (own, other)])
        tails = [jnp.sum(a[:, -8:].astype(f32), axis=0) for a in (own, other)]
        tails = jnp.concatenate(tails, axis=1)
        delta = jnp.where(core == 0, tails[0] + tails[1], tails[2] + tails[3])
        given = (q, grad, kv, jnp.broadcast_to(delta[None], (8, span)))
        wide = 128
    keep, give, stream, backward = call(
        functools.partial(softmax_kernel, (heads, planes, window, tok, aligned)),
        (idx, docs, *given, qkv, dec),
        (((half_keys, 2 * head), f32), ((half_keys, 2 * head), bf16), ((span, head), bf16), state),
        [
            pltpu.VMEM((2 * half_keys, wide), f32),
            pltpu.VMEM((2 * half_keys, span), bf16),
            pltpu.VMEM((2 * half_keys, span), bf16),
        ],
        flops=1 << 30,
    )
    after = [shift(backward, -k) for k in range(1, window)]
    taken = swap(give, 1)
    parts = (keep + taken.astype(f32)).astype(bf16).reshape(owners, window * rp, 2 * head)
    parts = lax.all_to_all(parts, "zx", 0, 0, tiled=True)

    square = [pltpu.VMEM((span, span), bf16)] * 2
    q_cot, k_part, v_part = call(
        functools.partial(linear_kernel, heads),
        (idx, docs, stream, qkv, dec, *before),
        (((span, head), bf16), ((span, head), f32), ((span, head), f32)),
        square,
        flops=1 << 28,
    )
    out = ((3 * tok, head), bf16)
    msgs = call(
        functools.partial(finish_kernel, heads),
        (idx, docs, q_cot, k_part, v_part, qkv, dec, *after),
        (out,) * heads,
        [pltpu.VMEM((span, head), bf16)] * 2,
    )
    msgs = [msgs[0]] + [swap(msgs[k], k) for k in range(1, heads)]
    whole = ((tok, heads * head), bf16)
    q_out, k_out, v_out = call(functools.partial(spread_kernel, heads), (idx, *msgs), (whole,) * 3)

    if aligned:
        one = ((tok, head), bf16)
        key_rows, value_rows = call(
            functools.partial(total_kernel, planes, xs, window), (parts,), (one, one)
        )
    else:
        split = parts.reshape(planes, xs, window, rp, 2 * head).astype(f32).sum(axis=1)
        total = sum(jnp.roll(split[:, window - 1 - j], -j, axis=0) for j in range(window))
        total = total.reshape(tok, 2 * head).astype(bf16)
        key_rows, value_rows = total[:, 0:head], total[:, head:]
    return key_rows, value_rows, q_out, k_out, v_out


def solution(mesh):
    groups, ctx = mesh.devices.shape
    fine = Mesh(mesh.devices.reshape(groups, ctx // 2, 2), ("groups", "zx", "core"))
    rows = P(("groups", "zx", "core"), None)
    return jax.shard_map(
        body,
        mesh=fine,
        in_specs=(rows,) * 9 + (P("groups"),),
        out_specs=(rows,) * 5,
        check_vma=False,
    )
```

time: 327 us -> 88.7 us (0.27)
  waiting for transfers between devices: 180 us -> 14.2 us
  blocking collectives: 64.7 us -> 25.6 us
  other arithmetic: 23.7 us -> 1.98 us
  Pallas kernels: 0 us -> 21.5 us
  matrix products: 19.4 us -> 0 us
  between operations: 16.7 us -> 0.76 us
  starting transfers between devices: 3.68 us -> 18.8 us
  local copies, waits for them, and re-layouts: 14.2 us -> 5.07 us
  loops' own time: 3.48 us -> 0 us
    all_gather x2 -> x0, waiting for transfers between devices: 100 us -> none  [entering(): gathered = jax.tree.map(lambda a: lax.all_gather(a, axis), part)]
    reduce_scatter x2 -> x0, waiting for transfers between devices: 71.8 us -> none  [the longest x1 58.8 us: body(): lax.psum_scatter(value_buffer, 'ctx', scatter_dimension=0, tiled=True)]
    all_gather x3 -> x0, blocking collectives: 64.7 us -> none  [the longest x1 26.3 us: body(): all_keys = lax.all_gather(softmax_key, 'ctx', axis=0, tiled=True)]
    all_to_all x0 -> x1, blocking collectives: none -> 25.6 us  [body(): own = lax.all_to_all(send, 'zx', 0, 0, tiled=True)]
    pallas_call x0 -> x8, Pallas kernels: none -> 21.5 us  [call(): pl.pallas_call(body, in_specs=in_specs, out_specs=tuple((VMEM for _ in ou...]
    dot_general x22 -> x0, matrix products: 19.4 us -> none  [the longest x2 4.53 us: tile_grads(): jnp.einsum('yrv,vg->yrg', score_gradient, key_tile_block, preferred_eleme...]
    add x25 -> x0, other arithmetic: 16 us -> none  [the longest x15 15.9 us: chain_join(): later[1] + later[0][:, None, None] * earlier[1]]
    ppermute x0 -> x12, starting transfers between devices: none -> 15.3 us  [the longest x4 10.7 us: shift(): return lax.ppermute(a, line, pairs)]
  transfers between devices with their start and end apart: 5 -> 13, of which waited for: 5 -> 6; matrix products, arithmetic and copies ran while one was open for 4% -> 1% of each run, Pallas kernels for 0% -> 13%
where the time goes in v1:
time: 88.7 us; the launch traced here: 88 us
  blocking collectives  25.6 us (29%)
  Pallas kernels  21.5 us (24%)
  starting transfers between devices  18.8 us (21%)
  waiting for transfers between devices  14.2 us (16%)
  local copies, waits for them, and re-layouts  5.07 us (6%)
  other arithmetic  1.98 us (2%)
    all_to_all x1, blocking collectives, body(): own = lax.all_to_all(send, 'zx', 0, 0, tiled=True)  25.6 us
    pallas_call x8, Pallas kernels, call(): pl.pallas_call(body, in_specs=in_specs, out_specs=tuple((VMEM for _ in ou...  21.5 us
    ppermute x8, waiting for transfers between devices, swap(): return lax.ppermute(a, line, [(i, i ^ k) for i in range(n)])  11.3 us
    ppermute x4, starting transfers between devices, shift(): return lax.ppermute(a, line, pairs)  10.7 us
    unnamed x33, local copies, waits for them, and re-layouts  5.07 us
    ppermute x8, starting transfers between devices, swap(): return lax.ppermute(a, line, [(i, i ^ k) for i in range(n)])  4.56 us
    all_to_all x1, starting transfers between devices, body(): parts = lax.all_to_all(parts, 'zx', 0, 0, tiled=True)  3.58 us
    ppermute x4, waiting for transfers between devices, shift(): return lax.ppermute(a, line, pairs)  2.93 us
  transfers between devices with their start and end apart: 13, of which 6 were waited for; matrix products, arithmetic and copies ran while one was open for 1% of the time, Pallas kernels for 13%

profile of v1, /device:TPU:0, one launch (start us, length us, event | category | flops | bytes accessed | tf_op | source)
XLA Modules:
  0.0 88.0 jit_solution(12854185069834918448)
XLA Ops:
  0.6 2.3 %shard_map.137 = bf16[8,168,256]{2,1,0:T(8,128)(2,1)} custom-call(s32[1]{0:T(128)} %bitcast.idx_ref.refs_0_, bf16[128,512]{1,0:T(8,128)(2,1)} %q_ref.2, bf16[128,128]{1,0:T(8,128)(2,1)} %k_ref.2, bf16[128,128]{1,0:T(8,128)(2,1)} %v_ref.2, bf16[128,512]{1,0:T(8,128)(2,1)} %o_ref.1, bf16[128,512]{1,0:T(8,128)(2,1)} %g_ref.1), custom_call_target="tpu_custom_call" | custom-call | flops 1048576 | bytes 1048576 | tf_op jit(solution)/shard_map/pallas_call | solution.py:384
  3.0 25.6 %all_to_all.10.refs_2_ = bf16[8,168,256]{2,1,0:T(8,128)(2,1)S(1)} all-to-all(bf16[8,168,256]{2,1,0:T(8,128)(2,1)} %shard_map.137), channel_id=1, replica_groups=mesh['groups'=2,'zx'=8,'core'=2] {'zx'}, dimensions={0} | all-to-all | bytes 1376256 | tf_op jit(solution)/shard_map/all_to_all | solution.py:446
  28.6 0.9 copy.15.dec_ref
  29.5 1.9 %shard_map.138 = (bf16[400,128]{1,0:T(8,128)(2,1)}, bf16[400,128]{1,0:T(8,128)(2,1)}, bf16[400,128]{1,0:T(8,128)(2,1)}, bf16[400,128]{1,0:T(8,128)(2,1)}) custom-call(s32[1]{0:T(128)} %bitcast.idx_ref.refs_0_, bf16[128,512]{1,0:T(8,128)(2,1)} %q_ref.3, bf16[128,512]{1,0:T(8,128)(2,1)} %k_ref.3, bf16[128,512]{1,0:T(8,128)(2,1)} %v_ref.3, f32[128,4]{1,0:T(8,128)} %copy.15.dec_ref), custom_call_target="tpu_custom_call" | custom-call | flops 1048576 | bytes 1048576 | tf_op jit(solution)/shard_map/pallas_call | solution.py:384
  31.7 1.2 %collective-permute-start.2 = (bf16[400,128]{1,0:T(8,128)(2,1)}, bf16[400,128]{1,0:T(8,128)(2,1)S(1)}, u32[]{:S(2)}, u32[]{:S(2)}) collective-permute-start(bf16[400,128]{1,0:T(8,128)(2,1)} %get-tuple-element.30), channel_id=1, source_target_pairs={{0,2},{1,3},{2,0},{3,1},{4,6},{5,7},{6,4},{7,5},{8,10},{9,11},{10,... | collective-permute-start | bytes 307208 | tf_op jit(solution)/shard_map/ppermute | solution.py:423
  33.2 4.4 %collective-permute-done.2.rest_2_ = bf16[400,128]{1,0:T(8,128)(2,1)S(1)} collective-permute-done((bf16[400,128]{1,0:T(8,128)(2,1)}, bf16[400,128]{1,0:T(8,128)(2,1)S(1)}, u32[]{:S(2)}, u32[]{:S(2)}) %collective-permute-start.2) | collective-permute-done | bytes 102432 | tf_op jit(solution)/shard_map/ppermute | solution.py:423
  39.0 2.1 %shard_map.139 = (bf16[3,512,128]{2,1,0:T(8,128)(2,1)}, f32[8,512]{1,0:T(8,128)}, f32[136,128]{1,0:T(8,128)}) custom-call(s32[1]{0:T(128)} %bitcast.idx_ref.refs_0_, s32[16,128]{1,0:T(8,128)} %bitcast.3, bf16[400,128]{1,0:T(8,128)(2,1)} %get-tuple-element.28.rest_0_, bf16[400,128]{1,0:T(8,128)(2,1)} %copy-done.2, bf16[400,128]{1,0:T(8,128)(2,1)} %copy-done.3, ...), custom_call_target="tpu_custom_call" | custom-call | flops 1048576 | bytes 1048576 | tf_op jit(solution)/shard_map/pallas_call | solution.py:384
  41.1 0.9 copy-done.11
  41.9 6.3 %shard_map.140 = (f32[768,256]{1,0:T(8,128)}, bf16[768,256]{1,0:T(8,128)(2,1)}, bf16[512,128]{1,0:T(8,128)(2,1)}, f32[136,128]{1,0:T(8,128)}) custom-call(s32[1]{0:T(128)} %bitcast.idx_ref.refs_0_, s32[16,128]{1,0:T(8,128)} %bitcast.4, bf16[8,168,256]{2,1,0:T(8,128)(2,1)} %copy-done.1, bf16[8,168,256]{2,1,0:T(8,128)(2,1)} %copy-done.11, ...), custom_call_target="tpu_custom_call" | custom-call | flops 1073741824 | bytes 1048576 | tf_op jit(solution)/shard_map/pallas_call | solution.py:384
  48.8 1.6 %collective-permute-done.4 = bf16[768,256]{1,0:T(8,128)(2,1)S(1)} collective-permute-done((bf16[768,256]{1,0:T(8,128)(2,1)}, bf16[768,256]{1,0:T(8,128)(2,1)S(1)}, u32[]{:S(2)}, u32[]{:S(2)}) %collective-permute-start.4) | collective-permute-done | bytes 393248 | tf_op jit(solution)/shard_map/ppermute | solution.py:423
  50.4 2.0 %add_convert_fusion = bf16[768,256]{1,0:T(8,128)(2,1)} fusion(f32[768,256]{1,0:T(8,128)} %get-tuple-element.34, bf16[768,256]{1,0:T(8,128)(2,1)S(1)} %collective-permute-done.4), kind=kLoop, calls=%fused_computation | loop fusion | flops 589824 | bytes 1572864 | tf_op jit(solution)/shard_map/convert_element_type | solution.py:484
  52.4 3.6 %all-to-all-start.1 = ((bf16[8,96,256]{2,1,0:T(8,128)(2,1)}), bf16[8,96,256]{2,1,0:T(8,128)(2,1)S(1)}, u32[]{:S(2)}, u32[]{:S(2)}) async-start(bf16[8,96,256]{2,1,0:T(8,128)(2,1)} %bitcast.2), calls=%async_computation.1 | async-start | bytes 786432 | tf_op jit(solution)/shard_map/all_to_all | solution.py:485
  56.0 3.8 %collective-permute-start.5 = (f32[136,128]{1,0:T(8,128)S(1)}, f32[136,128]{1,0:T(8,128)S(1)}, u32[]{:S(2)}, u32[]{:S(2)}) collective-permute-start(f32[136,128]{1,0:T(8,128)S(1)} %copy-done.13), channel_id=1, source_target_pairs={{0,4},{1,5},{2,6},{3,7},{4,8},{5,9},{6,10},{7,11},{8,12},{9,13},{1... | collective-permute-start | bytes 208904 | tf_op jit(solution)/shard_map/ppermute | solution.py:427
  59.8 4.3 %collective-permute-start.6 = (f32[136,128]{1,0:T(8,128)S(1)}, f32[136,128]{1,0:T(8,128)S(1)}, u32[]{:S(2)}, u32[]{:S(2)}) collective-permute-start(f32[136,128]{1,0:T(8,128)S(1)} %copy-done.13), channel_id=1, source_target_pairs={{0,8},{1,9},{2,10},{3,11},{4,12},{5,13},{6,14},{7,15},{16,24},{17,... | collective-permute-start | bytes 208904 | tf_op jit(solution)/shard_map/ppermute | solution.py:427
  64.1 1.3 %collective-permute-start.7 = (f32[136,128]{1,0:T(8,128)S(1)}, f32[136,128]{1,0:T(8,128)S(1)}, u32[]{:S(2)}, u32[]{:S(2)}) collective-permute-start(f32[136,128]{1,0:T(8,128)S(1)} %copy-done.12), channel_id=1, source_target_pairs={{4,0},{5,1},{6,2},{7,3},{8,4},{9,5},{10,6},{11,7},{12,8},{13,9},{1... | collective-permute-start | bytes 208904 | tf_op jit(solution)/shard_map/ppermute | solution.py:427
  65.4 1.3 %collective-permute-start.8 = (f32[136,128]{1,0:T(8,128)S(1)}, f32[136,128]{1,0:T(8,128)S(1)}, u32[]{:S(2)}, u32[]{:S(2)}) collective-permute-start(f32[136,128]{1,0:T(8,128)S(1)} %copy-done.12), channel_id=1, source_target_pairs={{8,0},{9,1},{10,2},{11,3},{12,4},{13,5},{14,6},{15,7},{24,16},{25,... | collective-permute-start | bytes 208904 | tf_op jit(solution)/shard_map/ppermute | solution.py:427
  67.4 3.0 %shard_map.142 = (bf16[512,128]{1,0:T(8,128)(2,1)}, f32[512,128]{1,0:T(8,128)}, f32[512,128]{1,0:T(8,128)}) custom-call(s32[1]{0:T(128)} %bitcast.idx_ref.refs_0_, s32[16,128]{1,0:T(8,128)} %bitcast.5, bf16[512,128]{1,0:T(8,128)(2,1)} %get-tuple-element.38.stream_ref, bf16[3,512,128]{2,1,0:T(8,128)(2,1)} %get-tuple-element.32.refs_4_.qkv, ...), custom_call_target="tpu_custom_call" | custom-call | flops 268435456 | bytes 1048576 | tf_op jit(solution)/shard_map/pallas_call | solution.py:384
  70.3 2.9 %collective-permute-done.8.rest_1_ = f32[136,128]{1,0:T(8,128)S(1)} collective-permute-done((f32[136,128]{1,0:T(8,128)S(1)}, f32[136,128]{1,0:T(8,128)S(1)}, u32[]{:S(2)}, u32[]{:S(2)}) %collective-permute-start.8) | collective-permute-done | bytes 69664 | tf_op jit(solution)/shard_map/ppermute | solution.py:427
  73.9 2.4 %shard_map.143 = (bf16[384,128]{1,0:T(8,128)(2,1)}, bf16[384,128]{1,0:T(8,128)(2,1)}, bf16[384,128]{1,0:T(8,128)(2,1)}, bf16[384,128]{1,0:T(8,128)(2,1)}) custom-call(s32[1]{0:T(128)} %bitcast.idx_ref.refs_0_, s32[16,128]{1,0:T(8,128)} %bitcast.6, bf16[512,128]{1,0:T(8,128)(2,1)} %get-tuple-element.40.q_ref, f32[512,128]{1,0:T(8,128)} %get-tuple-element.41.k_ref, ...), custom_call_target="tpu_custom_call" | custom-call | flops 1048576 | bytes 1048576 | tf_op jit(solution)/shard_map/pallas_call | solution.py:384
  76.3 1.5 %collective-permute-start.10 = (bf16[384,128]{1,0:T(8,128)(2,1)}, bf16[384,128]{1,0:T(8,128)(2,1)S(1)}, u32[]{:S(2)}, u32[]{:S(2)}) collective-permute-start(bf16[384,128]{1,0:T(8,128)(2,1)} %get-tuple-element.46), channel_id=1, source_target_pairs={{0,2},{1,3},{2,0},{3,1},{4,6},{5,7},{6,4},{7,5},{8,10},{9,11},{10,... | collective-permute-start | bytes 294920 | tf_op jit(solution)/shard_map/ppermute | solution.py:423
  78.4 2.8 %collective-permute-done.10.rest_2_ = bf16[384,128]{1,0:T(8,128)(2,1)S(1)} collective-permute-done((bf16[384,128]{1,0:T(8,128)(2,1)}, bf16[384,128]{1,0:T(8,128)(2,1)S(1)}, u32[]{:S(2)}, u32[]{:S(2)}) %collective-permute-start.10) | collective-permute-done | bytes 98336 | tf_op jit(solution)/shard_map/ppermute | solution.py:423
  81.3 1.8 %collective-permute-done.11.rest_3_ = bf16[384,128]{1,0:T(8,128)(2,1)S(1)} collective-permute-done((bf16[384,128]{1,0:T(8,128)(2,1)}, bf16[384,128]{1,0:T(8,128)(2,1)S(1)}, u32[]{:S(2)}, u32[]{:S(2)}) %collective-permute-start.11) | collective-permute-done | bytes 98336 | tf_op jit(solution)/shard_map/ppermute | solution.py:423
  83.7 1.8 %shard_map.144 = (bf16[128,512]{1,0:T(8,128)(2,1)}, bf16[128,512]{1,0:T(8,128)(2,1)}, bf16[128,512]{1,0:T(8,128)(2,1)}) custom-call(s32[1]{0:T(128)} %bitcast.idx_ref.refs_0_, bf16[384,128]{1,0:T(8,128)(2,1)} %get-tuple-element.44.rest_0_, bf16[384,128]{1,0:T(8,128)(2,1)} %copy-done.7, bf16[384,128]{1,0:T(8,128)(2,1)} %copy-done.5, bf16[384,128]{1,0:T(8,128)(2,1)} %copy-done.6), custom_call_target="tpu_custom_call" | custom-call | flops 1048576 | bytes 1048576 | tf_op jit(solution)/shard_map/pallas_call | solution.py:384
  86.3 1.7 %shard_map.141 = (bf16[128,128]{1,0:T(8,128)(2,1)}, bf16[128,128]{1,0:T(8,128)(2,1)}) custom-call(bf16[8,96,256]{2,1,0:T(8,128)(2,1)} %copy-done), custom_call_target="tpu_custom_call" | custom-call | flops 1048576 | bytes 1048576 | tf_op jit(solution)/shard_map/pallas_call | solution.py:384
  (45 shorter events, 6.0 us)
Async XLA Ops:
  3.0 25.7 %copy-start.10 = (f32[128,4]{0,1:T(4,128)S(1)}, f32[128,4]{0,1:T(4,128)}, u32[]{:S(2)}) copy-start(f32[128,4]{0,1:T(4,128)} %param.18) | copy-start | bytes 6148
  28.6 12.5 %copy-start.1 = (bf16[8,168,256]{2,1,0:T(8,128)(2,1)}, bf16[8,168,256]{2,1,0:T(8,128)(2,1)S(1)}, u32[]{:S(2)}) copy-start(bf16[8,168,256]{2,1,0:T(8,128)(2,1)S(1)} %all_to_all.10.refs_2_) | copy-start | bytes 2064388
  28.6 12.5 %collective-permute-start = (bf16[8,168,256]{2,1,0:T(8,128)(2,1)S(1)}, bf16[8,168,256]{2,1,0:T(8,128)(2,1)S(1)}, u32[]{:S(2)}, u32[]{:S(2)}) collective-permute-start(bf16[8,168,256]{2,1,0:T(8,128)(2,1)S(1)} %all_to_all.10.refs_2_), channel_id=1, source_target_pairs={{0,1},{1,0},{2,3},{3,2},{4,5},{5,4},{6,7},{7,6},{8,9},{9,8},{10,11... | collective-permute-start | bytes 2064392 | tf_op jit(solution)/shard_map/ppermute | solution.py:423
  31.4 1.9 %collective-permute-start.1 = (bf16[400,128]{1,0:T(8,128)(2,1)}, bf16[400,128]{1,0:T(8,128)(2,1)S(1)}, u32[]{:S(2)}, u32[]{:S(2)}) collective-permute-start(bf16[400,128]{1,0:T(8,128)(2,1)} %get-tuple-element.29), channel_id=1, source_target_pairs={{0,1},{1,0},{2,3},{3,2},{4,5},{5,4},{6,7},{7,6},{8,9},{9,8},{10,11... | collective-permute-start | bytes 307208 | tf_op jit(solution)/shard_map/ppermute | solution.py:423
  31.7 5.9 %collective-permute-start.2 = (bf16[400,128]{1,0:T(8,128)(2,1)}, bf16[400,128]{1,0:T(8,128)(2,1)S(1)}, u32[]{:S(2)}, u32[]{:S(2)}) collective-permute-start(bf16[400,128]{1,0:T(8,128)(2,1)} %get-tuple-element.30), channel_id=1, source_target_pairs={{0,2},{1,3},{2,0},{3,1},{4,6},{5,7},{6,4},{7,5},{8,10},{9,11},{10,... | collective-permute-start | bytes 307208 | tf_op jit(solution)/shard_map/ppermute | solution.py:423
  33.0 5.4 %collective-permute-start.3 = (bf16[400,128]{1,0:T(8,128)(2,1)}, bf16[400,128]{1,0:T(8,128)(2,1)S(1)}, u32[]{:S(2)}, u32[]{:S(2)}) collective-permute-start(bf16[400,128]{1,0:T(8,128)(2,1)} %get-tuple-element.31), channel_id=1, source_target_pairs={{0,3},{1,2},{2,1},{3,0},{4,7},{5,6},{6,5},{7,4},{8,11},{9,10},{10,... | collective-permute-start | bytes 307208 | tf_op jit(solution)/shard_map/ppermute | solution.py:423
  33.2 5.1 %copy-start.2 = (bf16[400,128]{1,0:T(8,128)(2,1)}, bf16[400,128]{1,0:T(8,128)(2,1)S(1)}, u32[]{:S(2)}) copy-start(bf16[400,128]{1,0:T(8,128)(2,1)S(1)} %collective-permute-done.1.rest_1_) | copy-start | bytes 307204
  37.6 0.7 copy-start.3
  41.1 0.9 copy-start.11
  48.3 2.1 %collective-permute-start.4 = (bf16[768,256]{1,0:T(8,128)(2,1)}, bf16[768,256]{1,0:T(8,128)(2,1)S(1)}, u32[]{:S(2)}, u32[]{:S(2)}) collective-permute-start(bf16[768,256]{1,0:T(8,128)(2,1)} %get-tuple-element.35), channel_id=1, source_target_pairs={{0,1},{1,0},{2,3},{3,2},{4,5},{5,4},{6,7},{7,6},{8,9},{9,8},{10,11... | collective-permute-start | bytes 1179656 | tf_op jit(solution)/shard_map/ppermute | solution.py:423
  52.4 3.6 %copy-start.13 = (f32[136,128]{1,0:T(8,128)S(1)}, f32[136,128]{1,0:T(8,128)}, u32[]{:S(2)}) copy-start(f32[136,128]{1,0:T(8,128)} %get-tuple-element.39) | copy-start | bytes 208900
  52.4 11.7 %copy-start.12 = (f32[136,128]{1,0:T(8,128)S(1)}, f32[136,128]{1,0:T(8,128)}, u32[]{:S(2)}) copy-start(f32[136,128]{1,0:T(8,128)} %get-tuple-element.43) | copy-start | bytes 208900
  52.4 33.2 %all-to-all-start.1 = ((bf16[8,96,256]{2,1,0:T(8,128)(2,1)}), bf16[8,96,256]{2,1,0:T(8,128)(2,1)S(1)}, u32[]{:S(2)}, u32[]{:S(2)}) async-start(bf16[8,96,256]{2,1,0:T(8,128)(2,1)} %bitcast.2), calls=%async_computation.1 | async-start | bytes 786432 | tf_op jit(solution)/shard_map/all_to_all | solution.py:485
  56.0 10.8 %collective-permute-start.5 = (f32[136,128]{1,0:T(8,128)S(1)}, f32[136,128]{1,0:T(8,128)S(1)}, u32[]{:S(2)}, u32[]{:S(2)}) collective-permute-start(f32[136,128]{1,0:T(8,128)S(1)} %copy-done.13), channel_id=1, source_target_pairs={{0,4},{1,5},{2,6},{3,7},{4,8},{5,9},{6,10},{7,11},{8,12},{9,13},{1... | collective-permute-start | bytes 208904 | tf_op jit(solution)/shard_map/ppermute | solution.py:427
  59.8 6.9 %collective-permute-start.6 = (f32[136,128]{1,0:T(8,128)S(1)}, f32[136,128]{1,0:T(8,128)S(1)}, u32[]{:S(2)}, u32[]{:S(2)}) collective-permute-start(f32[136,128]{1,0:T(8,128)S(1)} %copy-done.13), channel_id=1, source_target_pairs={{0,8},{1,9},{2,10},{3,11},{4,12},{5,13},{6,14},{7,15},{16,24},{17,... | collective-permute-start | bytes 208904 | tf_op jit(solution)/shard_map/ppermute | solution.py:427
  64.1 6.2 %collective-permute-start.7 = (f32[136,128]{1,0:T(8,128)S(1)}, f32[136,128]{1,0:T(8,128)S(1)}, u32[]{:S(2)}, u32[]{:S(2)}) collective-permute-start(f32[136,128]{1,0:T(8,128)S(1)} %copy-done.12), channel_id=1, source_target_pairs={{4,0},{5,1},{6,2},{7,3},{8,4},{9,5},{10,6},{11,7},{12,8},{13,9},{1... | collective-permute-start | bytes 208904 | tf_op jit(solution)/shard_map/ppermute | solution.py:427
  65.4 7.8 %collective-permute-start.8 = (f32[136,128]{1,0:T(8,128)S(1)}, f32[136,128]{1,0:T(8,128)S(1)}, u32[]{:S(2)}, u32[]{:S(2)}) collective-permute-start(f32[136,128]{1,0:T(8,128)S(1)} %copy-done.12), channel_id=1, source_target_pairs={{8,0},{9,1},{10,2},{11,3},{12,4},{13,5},{14,6},{15,7},{24,16},{25,... | collective-permute-start | bytes 208904 | tf_op jit(solution)/shard_map/ppermute | solution.py:427
  70.3 2.9 %copy-start.8 = (f32[136,128]{1,0:T(8,128)}, f32[136,128]{1,0:T(8,128)S(1)}, u32[]{:S(2)}) copy-start(f32[136,128]{1,0:T(8,128)S(1)} %collective-permute-done.7.rest_0_) | copy-start | bytes 208900
  76.3 5.0 %collective-permute-start.10 = (bf16[384,128]{1,0:T(8,128)(2,1)}, bf16[384,128]{1,0:T(8,128)(2,1)S(1)}, u32[]{:S(2)}, u32[]{:S(2)}) collective-permute-start(bf16[384,128]{1,0:T(8,128)(2,1)} %get-tuple-element.46), channel_id=1, source_target_pairs={{0,2},{1,3},{2,0},{3,1},{4,6},{5,7},{6,4},{7,5},{8,10},{9,11},{10,... | collective-permute-start | bytes 294920 | tf_op jit(solution)/shard_map/ppermute | solution.py:423
  77.7 5.3 %collective-permute-start.11 = (bf16[384,128]{1,0:T(8,128)(2,1)}, bf16[384,128]{1,0:T(8,128)(2,1)S(1)}, u32[]{:S(2)}, u32[]{:S(2)}) collective-permute-start(bf16[384,128]{1,0:T(8,128)(2,1)} %get-tuple-element.47), channel_id=1, source_target_pairs={{0,3},{1,2},{2,1},{3,0},{4,7},{5,6},{6,5},{7,4},{8,11},{9,10},{10,... | collective-permute-start | bytes 294920 | tf_op jit(solution)/shard_map/ppermute | solution.py:423
  77.7 5.3 %collective-permute-start.9 = (bf16[384,128]{1,0:T(8,128)(2,1)}, bf16[384,128]{1,0:T(8,128)(2,1)S(1)}, u32[]{:S(2)}, u32[]{:S(2)}) collective-permute-start(bf16[384,128]{1,0:T(8,128)(2,1)} %get-tuple-element.45), channel_id=1, source_target_pairs={{0,1},{1,0},{2,3},{3,2},{4,5},{5,4},{6,7},{7,6},{8,9},{9,8},{10,11... | collective-permute-start | bytes 294920 | tf_op jit(solution)/shard_map/ppermute | solution.py:423
  81.3 1.8 %copy-start.5 = (bf16[384,128]{1,0:T(8,128)(2,1)}, bf16[384,128]{1,0:T(8,128)(2,1)S(1)}, u32[]{:S(2)}) copy-start(bf16[384,128]{1,0:T(8,128)(2,1)S(1)} %collective-permute-done.10.rest_2_) | copy-start | bytes 294916
  83.0 0.7 copy-start.7
  85.6 0.7 copy-start
  (5 other events, 3.2 us)

commit v2 on v1

--- a/solution.py
+++ b/solution.py
@@ -13,6 +13,7 @@
 DEC_ROWS = 16
 VMEM = pl.BlockSpec(memory_space=pltpu.VMEM)
 SMEM = pl.BlockSpec(memory_space=pltpu.SMEM)
+HBM = pl.BlockSpec(memory_space=pltpu.HBM)
 
 
 def nt(a, b):
@@ -71,11 +72,9 @@
     return c_row, c_col
 
 
-def pack_linear(heads, idx_ref, q_ref, k_ref, v_ref, dec_ref, *rest):
-    outs, scr = rest[:heads], rest[heads]
+def pack_linear(heads, idx_ref, q_ref, k_ref, v_ref, dec_ref, outs):
     tok, head = q_ref.shape[0], q_ref.shape[1] // heads
     p = lax.rem(idx_ref[0], heads)
-    scr[...] = jnp.concatenate([dec_ref[...], jnp.zeros((tok, head - heads), f32)], axis=1).T
     for k in range(heads):
         h = p ^ k
         lanes = pl.ds(pl.multiple_of(h * head, head), head)
@@ -83,13 +82,12 @@
         out[0:tok, :] = q_ref[:, lanes]
         out[tok : 2 * tok, :] = k_ref[:, lanes]
         out[2 * tok : 3 * tok, :] = v_ref[:, lanes]
-        d = scr[pl.ds(h, 1), :]
-        hi = d.astype(bf16)
-        left = d - hi.astype(f32)
-        mid = left.astype(bf16)
-        low = (left - mid.astype(f32)).astype(bf16)
-        r = iota((DEC_ROWS, head), 0)
-        rows = jnp.where(r == 0, hi.astype(f32), jnp.where(r == 1, mid.astype(f32), jnp.where(r == 2, low.astype(f32), 0.0)))
+        d = dec_ref[pl.ds(h, 1), :]
+        hi = d.astype(bf16).astype(f32)
+        mid = (d - hi).astype(bf16).astype(f32)
+        low = d - hi - mid
+        r = iota((DEC_ROWS, tok), 0)
+        rows = jnp.where(r == 0, hi, jnp.where(r == 1, mid, jnp.where(r == 2, low, 0.0)))
         out[3 * tok : 3 * tok + DEC_ROWS, :] = rows.astype(bf16)
 
 
@@ -123,6 +121,20 @@
             out[to, (2 + window) * rp : (2 + window) * rp + 8, :] = tail.astype(bf16)
 
 
+def pack_kernel(heads, planes, window, count, idx_ref, *refs):
+    ins, outs, held, sem = refs[:count], refs[count : -count - 1], refs[-count - 1 : -1], refs[-1]
+    copies = [pltpu.make_async_copy(a, b, sem.at[i]) for i, (a, b) in enumerate(zip(ins, held))]
+    for c in copies:
+        c.start()
+    for c in copies[-4:]:
+        c.wait()
+    pack_linear(heads, idx_ref, *held[-4:], outs[-heads:])
+    if window:
+        for c in copies[:-4]:
+            c.wait()
+        pack_main(heads, planes, window, idx_ref, *held[:5], outs[0])
+
+
 def pack_main_plain(heads, planes, window, idx, q, k, v, o, grad):
     tok, head = k.shape
     rp, xs = tok // planes, heads // 2
@@ -379,15 +391,15 @@
         v_out[rows, :] = total[:, head : 2 * head].astype(bf16)
 
 
-def call(body, ins, outs, scratch=(), flops=1 << 20):
-    in_specs = [SMEM if a.dtype == i32 and a.ndim == 1 else VMEM for a in ins]
+def call(body, ins, outs, scratch=(), flops=1 << 20, grant=8, space=VMEM):
+    in_specs = [SMEM if a.dtype == i32 and a.ndim == 1 else space for a in ins]
     return pl.pallas_call(
         body,
         in_specs=in_specs,
         out_specs=tuple(VMEM for _ in outs),
         out_shape=tuple(jax.ShapeDtypeStruct(*o) for o in outs),
         scratch_shapes=list(scratch),
-        compiler_params=pltpu.CompilerParams(vmem_limit_bytes=60000 * 1024),
+        compiler_params=pltpu.CompilerParams(vmem_limit_bytes=grant << 20),
         cost_estimate=pl.CostEstimate(flops=flops, bytes_accessed=1 << 20, transcendentals=0),
     )(*ins)
 
@@ -427,24 +439,28 @@
         return lax.ppermute(a, line, pairs)
 
     msg = ((3 * tok + DEC_ROWS, head), bf16)
-    lin = call(
-        functools.partial(pack_linear, heads),
-        (idx, linear_query, linear_key, linear_value, linear_decay),
-        (msg,) * heads,
-        [pltpu.VMEM((head, tok), f32)],
-    )
-    lin = [lin[0]] + [swap(lin[k], k) for k in range(1, heads)]
-
-    packed = (idx, softmax_query, softmax_key, softmax_value, softmax_output, upstream_grad)
+    packed = (softmax_query, softmax_key, softmax_value, softmax_output, upstream_grad)
+    linear = (linear_query, linear_key, linear_value, linear_decay.T)
     if aligned:
         rows = (2 + window) * rp + 8
-        send = call(
-            functools.partial(pack_main, heads, planes, window), packed, (((owners, rows, 2 * head), bf16),)
-        )[0]
-    else:
-        send = pack_main_plain(heads, planes, window, *packed)
+        send, *lin = call(
+            functools.partial(pack_kernel, heads, planes, window, 9),
+            (idx, *packed, *linear),
+            (((owners, rows, 2 * head), bf16),) + (msg,) * heads,
+            [pltpu.VMEM(a.shape, a.dtype) for a in (*packed, *linear)] + [pltpu.SemaphoreType.DMA((9,))],
+            space=HBM,
+        )
+    else:
+        send = pack_main_plain(heads, planes, window, idx, *packed)
+        lin = call(
+            functools.partial(pack_kernel, heads, planes, 0, 4),
+            (idx, *linear),
+            (msg,) * heads,
+            [pltpu.VMEM(a.shape, a.dtype) for a in linear] + [pltpu.SemaphoreType.DMA((4,))],
+            space=HBM,
+        )
     own = lax.all_to_all(send, "zx", 0, 0, tiled=True)
-    other = swap(own, 1)
+    lin = [lin[0]] + [swap(lin[k], k) for k in range(1, heads)]
 
     state = ((head + 8, head), f32)
     qkv, dec, forward = call(
@@ -452,7 +468,9 @@
         (idx, docs, *lin),
         (((3, span, head), bf16), ((8, span), f32), state),
     )
+    own, forward = lax.optimization_barrier((own, forward))
     before = [shift(forward, k) for k in range(1, window)]
+    other = swap(own, 1)
 
     if aligned:
         given = (own, other)
@@ -478,12 +496,10 @@
             pltpu.VMEM((2 * half_keys, span), bf16),
         ],
         flops=1 << 30,
+        grant=24 if aligned else 58,
     )
+    taken = swap(give, 1)
     after = [shift(backward, -k) for k in range(1, window)]
-    taken = swap(give, 1)
-    parts = (keep + taken.astype(f32)).astype(bf16).reshape(owners, window * rp, 2 * head)
-    parts = lax.all_to_all(parts, "zx", 0, 0, tiled=True)
-
     square = [pltpu.VMEM((span, span), bf16)] * 2
     q_cot, k_part, v_part = call(
         functools.partial(linear_kernel, heads),
@@ -491,7 +507,12 @@
         (((span, head), bf16), ((span, head), f32), ((span, head), f32)),
         square,
         flops=1 << 28,
+        grant=16,
     )
+    taken, k_part, *after = lax.optimization_barrier((taken, k_part, *after))
+    parts = (keep + taken.astype(f32)).astype(bf16).reshape(owners, window * rp, 2 * head)
+    parts = lax.all_to_all(parts, "zx", 0, 0, tiled=True)
+
     out = ((3 * tok, head), bf16)
     msgs = call(
         functools.partial(finish_kernel, heads),

time: 88.7 us -> 74 us (0.83)
  blocking collectives: 25.6 us -> 0 us
  waiting for transfers between devices: 14.2 us -> 29.8 us
  Pallas kernels: 21.5 us -> 9.94 us
  starting transfers between devices: 18.8 us -> 24.4 us
  local copies, waits for them, and re-layouts: 5.07 us -> 7.62 us
  other arithmetic: 1.98 us -> 0.88 us
    all_to_all x1 -> x0, blocking collectives: 25.6 us -> none  [body(): own = lax.all_to_all(send, 'zx', 0, 0, tiled=True)]
    pallas_call x8 -> x7, Pallas kernels: 21.5 us -> 9.94 us  [call(): pl.pallas_call(body, in_specs=in_specs, out_specs=tuple((VMEM for _ in ou...]
    all_to_all x0 -> x1, starting transfers between devices: none -> 7.29 us  [body(): own = lax.all_to_all(send, 'zx', 0, 0, tiled=True)]
    ppermute x8, waiting for transfers between devices: 11.3 us -> 17.8 us  [swap(): return lax.ppermute(a, line, [(i, i ^ k) for i in range(n)])]
    all_to_all x0 -> x1, waiting for transfers between devices: none -> 6.15 us  [body(): own = lax.all_to_all(send, 'zx', 0, 0, tiled=True)]
    ppermute x4, starting transfers between devices: 10.7 us -> 8.13 us  [shift(): return lax.ppermute(a, line, pairs)]
    unnamed x33 -> x20, local copies, waits for them, and re-layouts: 5.07 us -> 7.62 us
    ppermute x4, waiting for transfers between devices: 2.93 us -> 5.4 us  [shift(): return lax.ppermute(a, line, pairs)]
  transfers between devices with their start and end apart: 13 -> 14, of which waited for: 6 -> 8; matrix products, arithmetic and copies ran while one was open for 1% -> 0% of each run, Pallas kernels for 13% -> 4%
where the time goes in v2:
time: 74 us; the launch traced here: 73.4 us
  waiting for transfers between devices  29.8 us (40%)
  starting transfers between devices  24.4 us (33%)
  Pallas kernels  9.94 us (13%)
  local copies, waits for them, and re-layouts  7.62 us (10%)
  other arithmetic  0.88 us (1%)
  between operations  0.76 us (1%)
    ppermute x8, waiting for transfers between devices, swap(): return lax.ppermute(a, line, [(i, i ^ k) for i in range(n)])  17.8 us
    pallas_call x7, Pallas kernels, call(): pl.pallas_call(body, in_specs=in_specs, out_specs=tuple((VMEM for _ in ou...  9.94 us
    ppermute x4, starting transfers between devices, shift(): return lax.ppermute(a, line, pairs)  8.13 us
    unnamed x20, local copies, waits for them, and re-layouts  7.62 us
    all_to_all x1, starting transfers between devices, body(): own = lax.all_to_all(send, 'zx', 0, 0, tiled=True)  7.29 us
    all_to_all x1, waiting for transfers between devices, body(): own = lax.all_to_all(send, 'zx', 0, 0, tiled=True)  6.15 us
    ppermute x4, waiting for transfers between devices, shift(): return lax.ppermute(a, line, pairs)  5.4 us
    ppermute x8, starting transfers between devices, swap(): return lax.ppermute(a, line, [(i, i ^ k) for i in range(n)])  4.61 us
  transfers between devices with their start and end apart: 14, of which 8 were waited for; matrix products, arithmetic and copies ran while one was open for 0% of the time, Pallas kernels for 4%

profile of v2, /device:TPU:0, one launch (start us, length us, event | category | flops | bytes accessed | tf_op | source)
XLA Modules:
  0.0 73.4 jit_solution(16362717869494309990)
XLA Ops:
  1.3 0.9 %copy-done = bf16[128,512]{1,0:T(8,128)(2,1)S(1)} copy-done((bf16[128,512]{1,0:T(8,128)(2,1)S(1)}, bf16[128,512]{1,0:T(8,128)(2,1)}, u32[]{:S(2)}) %copy-start) | copy-done | bytes 131096
  2.2 0.9 %copy-done.1 = bf16[128,512]{1,0:T(8,128)(2,1)S(1)} copy-done((bf16[128,512]{1,0:T(8,128)(2,1)S(1)}, bf16[128,512]{1,0:T(8,128)(2,1)}, u32[]{:S(2)}) %copy-start.1) | copy-done | bytes 131096
  3.1 0.9 %copy-done.2 = bf16[128,512]{1,0:T(8,128)(2,1)S(1)} copy-done((bf16[128,512]{1,0:T(8,128)(2,1)S(1)}, bf16[128,512]{1,0:T(8,128)(2,1)}, u32[]{:S(2)}) %copy-start.2) | copy-done | bytes 131096
  4.0 0.9 %copy-done.3 = bf16[128,512]{1,0:T(8,128)(2,1)S(1)} copy-done((bf16[128,512]{1,0:T(8,128)(2,1)S(1)}, bf16[128,512]{1,0:T(8,128)(2,1)}, u32[]{:S(2)}) %copy-start.3) | copy-done | bytes 131096
  4.9 0.9 %copy-done.4 = bf16[128,512]{1,0:T(8,128)(2,1)S(1)} copy-done((bf16[128,512]{1,0:T(8,128)(2,1)S(1)}, bf16[128,512]{1,0:T(8,128)(2,1)}, u32[]{:S(2)}) %copy-start.4) | copy-done | bytes 131096
  5.8 0.9 %copy-done.5 = bf16[128,512]{1,0:T(8,128)(2,1)S(1)} copy-done((bf16[128,512]{1,0:T(8,128)(2,1)S(1)}, bf16[128,512]{1,0:T(8,128)(2,1)}, u32[]{:S(2)}) %copy-start.5) | copy-done | bytes 131096
  8.3 2.5 %shard_map.137 = (bf16[8,168,256]{2,1,0:T(8,128)(2,1)}, bf16[400,128]{1,0:T(8,128)(2,1)S(1)}, bf16[400,128]{1,0:T(8,128)(2,1)S(1)}, bf16[400,128]{1,0:T(8,128)(2,1)S(1)}, bf16[400,128]{1,0:T(8,128)(2,1)S(1)}) custom-call(s32[1]{0:T(128)} %bitcast.idx_ref.refs_0_, bf16[128,512]{1,0:T(8,128)(2,1)S(1)} %copy-done, bf16[128,128]{1,0:T(8,128)(2,1)S(1)} %copy-done.7, ...), custom_call_target="tpu_custom_call" | custom-call | flops 1048576 | bytes 1048576 | tf_op jit(solution)/shard_map/pallas_call | solution.py:396
  10.8 7.3 %all-to-all-start = ((bf16[8,168,256]{2,1,0:T(8,128)(2,1)}), bf16[8,168,256]{2,1,0:T(8,128)(2,1)S(1)}, u32[]{:S(2)}, u32[]{:S(2)}) async-start(bf16[8,168,256]{2,1,0:T(8,128)(2,1)} %get-tuple-element.35), calls=%async_computation | async-start | bytes 1376256 | tf_op jit(solution)/shard_map/all_to_all | solution.py:462
  18.1 2.0 %collective-permute-start.1 = (bf16[400,128]{1,0:T(8,128)(2,1)S(1)}, bf16[400,128]{1,0:T(8,128)(2,1)S(1)}, u32[]{:S(2)}, u32[]{:S(2)}) collective-permute-start(bf16[400,128]{1,0:T(8,128)(2,1)S(1)} %get-tuple-element.38), channel_id=1, source_target_pairs={{0,2},{1,3},{2,0},{3,1},{4,6},{5,7},{6,4},{7,5},{8,10},{9,11},{10,... | collective-permute-start | bytes 307208 | tf_op jit(solution)/shard_map/ppermute | solution.py:435
  20.2 9.3 %collective-permute-done.1.rest_2_ = bf16[400,128]{1,0:T(8,128)(2,1)S(1)} collective-permute-done((bf16[400,128]{1,0:T(8,128)(2,1)S(1)}, bf16[400,128]{1,0:T(8,128)(2,1)S(1)}, u32[]{:S(2)}, u32[]{:S(2)}) %collective-permute-start.1) | collective-permute-done | bytes 102432 | tf_op jit(solution)/shard_map/ppermute | solution.py:435
  29.9 6.1 %all-to-all-done.refs_2_ = bf16[8,168,256]{2,1,0:T(8,128)(2,1)S(1)} async-done(((bf16[8,168,256]{2,1,0:T(8,128)(2,1)}), bf16[8,168,256]{2,1,0:T(8,128)(2,1)S(1)}, u32[]{:S(2)}, u32[]{:S(2)}) %all-to-all-start) | async-done | bytes 688160 | tf_op jit(solution)/shard_map/all_to_all | solution.py:462
  36.1 2.1 %collective-permute-done.3.refs_3_ = bf16[8,168,256]{2,1,0:T(8,128)(2,1)S(1)} collective-permute-done((bf16[8,168,256]{2,1,0:T(8,128)(2,1)S(1)}, bf16[8,168,256]{2,1,0:T(8,128)(2,1)S(1)}, u32[]{:S(2)}, u32[]{:S(2)}) %collective-permute-start.3) | collective-permute-done | bytes 688160 | tf_op jit(solution)/shard_map/ppermute | solution.py:435
  38.2 4.1 %shard_map.139 = (f32[768,256]{1,0:T(8,128)S(1)}, bf16[768,256]{1,0:T(8,128)(2,1)S(1)}, bf16[512,128]{1,0:T(8,128)(2,1)S(1)}, f32[136,128]{1,0:T(8,128)S(1)}) custom-call(s32[1]{0:T(128)} %bitcast.idx_ref.refs_0_, s32[16,128]{1,0:T(8,128)S(1)} %bitcast.5, bf16[8,168,256]{2,1,0:T(8,128)(2,1)S(1)} %all-to-all-done.refs_2_, ...), custom_call_target="tpu_custom_call" | custom-call | flops 1073741824 | bytes 1048576 | tf_op jit(solution)/shard_map/pallas_call | solution.py:396
  42.5 2.4 %collective-permute-start.5 = (f32[136,128]{1,0:T(8,128)S(1)}, f32[136,128]{1,0:T(8,128)S(1)}, u32[]{:S(2)}, u32[]{:S(2)}) collective-permute-start(f32[136,128]{1,0:T(8,128)S(1)} %get-tuple-element.47), channel_id=1, source_target_pairs={{0,4},{1,5},{2,6},{3,7},{4,8},{5,9},{6,10},{7,11},{8,12},{9,13},{1... | collective-permute-start | bytes 208904 | tf_op jit(solution)/shard_map/ppermute | solution.py:439
  44.9 3.1 %collective-permute-start.6 = (f32[136,128]{1,0:T(8,128)S(1)}, f32[136,128]{1,0:T(8,128)S(1)}, u32[]{:S(2)}, u32[]{:S(2)}) collective-permute-start(f32[136,128]{1,0:T(8,128)S(1)} %get-tuple-element.47), channel_id=1, source_target_pairs={{0,8},{1,9},{2,10},{3,11},{4,12},{5,13},{6,14},{7,15},{16,24},{17,... | collective-permute-start | bytes 208904 | tf_op jit(solution)/shard_map/ppermute | solution.py:439
  48.0 1.3 %collective-permute-start.7 = (f32[136,128]{1,0:T(8,128)S(1)}, f32[136,128]{1,0:T(8,128)S(1)}, u32[]{:S(2)}, u32[]{:S(2)}) collective-permute-start(f32[136,128]{1,0:T(8,128)S(1)} %get-tuple-element.49), channel_id=1, source_target_pairs={{4,0},{5,1},{6,2},{7,3},{8,4},{9,5},{10,6},{11,7},{12,8},{13,9},{1... | collective-permute-start | bytes 208904 | tf_op jit(solution)/shard_map/ppermute | solution.py:439
  49.3 1.3 %collective-permute-start.8 = (f32[136,128]{1,0:T(8,128)S(1)}, f32[136,128]{1,0:T(8,128)S(1)}, u32[]{:S(2)}, u32[]{:S(2)}) collective-permute-start(f32[136,128]{1,0:T(8,128)S(1)} %get-tuple-element.49), channel_id=1, source_target_pairs={{8,0},{9,1},{10,2},{11,3},{12,4},{13,5},{14,6},{15,7},{24,16},{25,... | collective-permute-start | bytes 208904 | tf_op jit(solution)/shard_map/ppermute | solution.py:439
  50.7 1.1 %shard_map.140 = (bf16[512,128]{1,0:T(8,128)(2,1)S(1)}, f32[512,128]{1,0:T(8,128)S(1)}, f32[512,128]{1,0:T(8,128)S(1)}) custom-call(s32[1]{0:T(128)} %bitcast.idx_ref.refs_0_, s32[16,128]{1,0:T(8,128)S(1)} %bitcast.6, bf16[512,128]{1,0:T(8,128)(2,1)S(1)} %get-tuple-element.46.stream_ref, bf16[3,512,128]{2,1,0:T(8,128)(2,1)S(1)} %get-tuple-element.42.refs_4_.qkv, ...), custom_call_target="tpu_custom_call" | custom-call | flops 268435456 | bytes 1048576 | tf_op jit(solution)/shard_map/pallas_call | solution.py:396
  51.8 2.4 %collective-permute-done.7.rest_0_ = f32[136,128]{1,0:T(8,128)S(1)} collective-permute-done((f32[136,128]{1,0:T(8,128)S(1)}, f32[136,128]{1,0:T(8,128)S(1)}, u32[]{:S(2)}, u32[]{:S(2)}) %collective-permute-start.7) | collective-permute-done | bytes 69664 | tf_op jit(solution)/shard_map/ppermute | solution.py:439
  54.3 2.9 %collective-permute-done.8.rest_1_ = f32[136,128]{1,0:T(8,128)S(1)} collective-permute-done((f32[136,128]{1,0:T(8,128)S(1)}, f32[136,128]{1,0:T(8,128)S(1)}, u32[]{:S(2)}, u32[]{:S(2)}) %collective-permute-start.8) | collective-permute-done | bytes 69664 | tf_op jit(solution)/shard_map/ppermute | solution.py:439
  58.1 4.3 %all-to-all-start.1 = ((bf16[8,96,256]{2,1,0:T(8,128)(2,1)}), bf16[8,96,256]{2,1,0:T(8,128)(2,1)S(1)}, u32[]{:S(2)}, u32[]{:S(2)}) async-start(bf16[8,96,256]{2,1,0:T(8,128)(2,1)} %bitcast.3), calls=%async_computation.1 | async-start | bytes 786432 | tf_op jit(solution)/shard_map/all_to_all | solution.py:514
  62.8 2.1 %collective-permute-start.10 = (bf16[384,128]{1,0:T(8,128)(2,1)S(1)}, bf16[384,128]{1,0:T(8,128)(2,1)S(1)}, u32[]{:S(2)}, u32[]{:S(2)}) collective-permute-start(bf16[384,128]{1,0:T(8,128)(2,1)S(1)} %get-tuple-element.60), channel_id=1, source_target_pairs={{0,2},{1,3},{2,0},{3,1},{4,6},{5,7},{6,4},{7,5},{8,10},{9,11},{10,... | collective-permute-start | bytes 294920 | tf_op jit(solution)/shard_map/ppermute | solution.py:435
  65.1 3.7 %collective-permute-done.10.rest_2_ = bf16[384,128]{1,0:T(8,128)(2,1)S(1)} collective-permute-done((bf16[384,128]{1,0:T(8,128)(2,1)S(1)}, bf16[384,128]{1,0:T(8,128)(2,1)S(1)}, u32[]{:S(2)}, u32[]{:S(2)}) %collective-permute-start.10) | collective-permute-done | bytes 98336 | tf_op jit(solution)/shard_map/ppermute | solution.py:435
  68.8 2.7 %collective-permute-done.11.rest_3_ = bf16[384,128]{1,0:T(8,128)(2,1)S(1)} collective-permute-done((bf16[384,128]{1,0:T(8,128)(2,1)S(1)}, bf16[384,128]{1,0:T(8,128)(2,1)S(1)}, u32[]{:S(2)}, u32[]{:S(2)}) %collective-permute-start.11) | collective-permute-done | bytes 98336 | tf_op jit(solution)/shard_map/ppermute | solution.py:435
  (32 shorter events, 6.3 us)
Async XLA Ops:
  0.6 0.7 copy-start.9
  1.3 0.9 %copy-start = (bf16[128,512]{1,0:T(8,128)(2,1)S(1)}, bf16[128,512]{1,0:T(8,128)(2,1)}, u32[]{:S(2)}) copy-start(bf16[128,512]{1,0:T(8,128)(2,1)} %refs_0_.1) | copy-start | bytes 393220
  2.2 0.9 %copy-start.1 = (bf16[128,512]{1,0:T(8,128)(2,1)S(1)}, bf16[128,512]{1,0:T(8,128)(2,1)}, u32[]{:S(2)}) copy-start(bf16[128,512]{1,0:T(8,128)(2,1)} %refs_3_.1) | copy-start | bytes 393220
  3.1 0.9 %copy-start.2 = (bf16[128,512]{1,0:T(8,128)(2,1)S(1)}, bf16[128,512]{1,0:T(8,128)(2,1)}, u32[]{:S(2)}) copy-start(bf16[128,512]{1,0:T(8,128)(2,1)} %refs_4_.1) | copy-start | bytes 393220
  4.0 0.9 %copy-start.3 = (bf16[128,512]{1,0:T(8,128)(2,1)S(1)}, bf16[128,512]{1,0:T(8,128)(2,1)}, u32[]{:S(2)}) copy-start(bf16[128,512]{1,0:T(8,128)(2,1)} %refs_5_.1) | copy-start | bytes 393220
  4.9 0.9 %copy-start.4 = (bf16[128,512]{1,0:T(8,128)(2,1)S(1)}, bf16[128,512]{1,0:T(8,128)(2,1)}, u32[]{:S(2)}) copy-start(bf16[128,512]{1,0:T(8,128)(2,1)} %refs_6_.1) | copy-start | bytes 393220
  5.8 0.9 %copy-start.5 = (bf16[128,512]{1,0:T(8,128)(2,1)S(1)}, bf16[128,512]{1,0:T(8,128)(2,1)}, u32[]{:S(2)}) copy-start(bf16[128,512]{1,0:T(8,128)(2,1)} %refs_7_.1) | copy-start | bytes 393220
  6.8 0.8 %copy-start.7 = (bf16[128,128]{1,0:T(8,128)(2,1)S(1)}, bf16[128,128]{1,0:T(8,128)(2,1)}, u32[]{:S(2)}) copy-start(bf16[128,128]{1,0:T(8,128)(2,1)} %refs_1_.1) | copy-start | bytes 98308
  7.5 0.8 %copy-start.8 = (bf16[128,128]{1,0:T(8,128)(2,1)S(1)}, bf16[128,128]{1,0:T(8,128)(2,1)}, u32[]{:S(2)}) copy-start(bf16[128,128]{1,0:T(8,128)(2,1)} %refs_2_.1) | copy-start | bytes 98308
  10.8 25.3 %all-to-all-start = ((bf16[8,168,256]{2,1,0:T(8,128)(2,1)}), bf16[8,168,256]{2,1,0:T(8,128)(2,1)S(1)}, u32[]{:S(2)}, u32[]{:S(2)}) async-start(bf16[8,168,256]{2,1,0:T(8,128)(2,1)} %get-tuple-element.35), calls=%async_computation | async-start | bytes 1376256 | tf_op jit(solution)/shard_map/all_to_all | solution.py:462
  18.1 11.5 %copy-start.6 = (s32[2048]{0:T(1024)S(1)}, s32[2048]{0:T(1024)}, u32[]{:S(2)}) copy-start(s32[2048]{0:T(1024)} %param.19) | copy-start | bytes 24580
  18.1 2.1 %collective-permute-start = (bf16[400,128]{1,0:T(8,128)(2,1)S(1)}, bf16[400,128]{1,0:T(8,128)(2,1)S(1)}, u32[]{:S(2)}, u32[]{:S(2)}) collective-permute-start(bf16[400,128]{1,0:T(8,128)(2,1)S(1)} %get-tuple-element.37), channel_id=1, source_target_pairs={{0,1},{1,0},{2,3},{3,2},{4,5},{5,4},{6,7},{7,6},{8,9},{9,8},{10,11... | collective-permute-start | bytes 307208 | tf_op jit(solution)/shard_map/ppermute | solution.py:435
  18.1 11.4 %collective-permute-start.1 = (bf16[400,128]{1,0:T(8,128)(2,1)S(1)}, bf16[400,128]{1,0:T(8,128)(2,1)S(1)}, u32[]{:S(2)}, u32[]{:S(2)}) collective-permute-start(bf16[400,128]{1,0:T(8,128)(2,1)S(1)} %get-tuple-element.38), channel_id=1, source_target_pairs={{0,2},{1,3},{2,0},{3,1},{4,6},{5,7},{6,4},{7,5},{8,10},{9,11},{10,... | collective-permute-start | bytes 307208 | tf_op jit(solution)/shard_map/ppermute | solution.py:435
  20.1 9.4 %collective-permute-start.2 = (bf16[400,128]{1,0:T(8,128)(2,1)S(1)}, bf16[400,128]{1,0:T(8,128)(2,1)S(1)}, u32[]{:S(2)}, u32[]{:S(2)}) collective-permute-start(bf16[400,128]{1,0:T(8,128)(2,1)S(1)} %get-tuple-element.39), channel_id=1, source_target_pairs={{0,3},{1,2},{2,1},{3,0},{4,7},{5,6},{6,5},{7,4},{8,11},{9,10},{10,... | collective-permute-start | bytes 307208 | tf_op jit(solution)/shard_map/ppermute | solution.py:435
  36.0 2.1 %collective-permute-start.3 = (bf16[8,168,256]{2,1,0:T(8,128)(2,1)S(1)}, bf16[8,168,256]{2,1,0:T(8,128)(2,1)S(1)}, u32[]{:S(2)}, u32[]{:S(2)}) collective-permute-start(bf16[8,168,256]{2,1,0:T(8,128)(2,1)S(1)} %all-to-all-done.refs_2_), channel_id=1, source_target_pairs={{0,1},{1,0},{2,3},{3,2},{4,5},{5,4},{6,7},{7,6},{8,9},{9,8},{10,11... | collective-permute-start | bytes 2064392 | tf_op jit(solution)/shard_map/ppermute | solution.py:435
  42.3 14.9 %collective-permute-start.4 = (bf16[768,256]{1,0:T(8,128)(2,1)S(1)}, bf16[768,256]{1,0:T(8,128)(2,1)S(1)}, u32[]{:S(2)}, u32[]{:S(2)}) collective-permute-start(bf16[768,256]{1,0:T(8,128)(2,1)S(1)} %get-tuple-element.45), channel_id=1, source_target_pairs={{0,1},{1,0},{2,3},{3,2},{4,5},{5,4},{6,7},{7,6},{8,9},{9,8},{10,11... | collective-permute-start | bytes 1179656 | tf_op jit(solution)/shard_map/ppermute | solution.py:435
  42.5 8.2 %collective-permute-start.5 = (f32[136,128]{1,0:T(8,128)S(1)}, f32[136,128]{1,0:T(8,128)S(1)}, u32[]{:S(2)}, u32[]{:S(2)}) collective-permute-start(f32[136,128]{1,0:T(8,128)S(1)} %get-tuple-element.47), channel_id=1, source_target_pairs={{0,4},{1,5},{2,6},{3,7},{4,8},{5,9},{6,10},{7,11},{8,12},{9,13},{1... | collective-permute-start | bytes 208904 | tf_op jit(solution)/shard_map/ppermute | solution.py:439
  44.9 5.7 %collective-permute-start.6 = (f32[136,128]{1,0:T(8,128)S(1)}, f32[136,128]{1,0:T(8,128)S(1)}, u32[]{:S(2)}, u32[]{:S(2)}) collective-permute-start(f32[136,128]{1,0:T(8,128)S(1)} %get-tuple-element.47), channel_id=1, source_target_pairs={{0,8},{1,9},{2,10},{3,11},{4,12},{5,13},{6,14},{7,15},{16,24},{17,... | collective-permute-start | bytes 208904 | tf_op jit(solution)/shard_map/ppermute | solution.py:439
  48.0 6.2 %collective-permute-start.7 = (f32[136,128]{1,0:T(8,128)S(1)}, f32[136,128]{1,0:T(8,128)S(1)}, u32[]{:S(2)}, u32[]{:S(2)}) collective-permute-start(f32[136,128]{1,0:T(8,128)S(1)} %get-tuple-element.49), channel_id=1, source_target_pairs={{4,0},{5,1},{6,2},{7,3},{8,4},{9,5},{10,6},{11,7},{12,8},{13,9},{1... | collective-permute-start | bytes 208904 | tf_op jit(solution)/shard_map/ppermute | solution.py:439
  49.3 7.8 %collective-permute-start.8 = (f32[136,128]{1,0:T(8,128)S(1)}, f32[136,128]{1,0:T(8,128)S(1)}, u32[]{:S(2)}, u32[]{:S(2)}) collective-permute-start(f32[136,128]{1,0:T(8,128)S(1)} %get-tuple-element.49), channel_id=1, source_target_pairs={{8,0},{9,1},{10,2},{11,3},{12,4},{13,5},{14,6},{15,7},{24,16},{25,... | collective-permute-start | bytes 208904 | tf_op jit(solution)/shard_map/ppermute | solution.py:439
  58.1 14.7 %all-to-all-start.1 = ((bf16[8,96,256]{2,1,0:T(8,128)(2,1)}), bf16[8,96,256]{2,1,0:T(8,128)(2,1)S(1)}, u32[]{:S(2)}, u32[]{:S(2)}) async-start(bf16[8,96,256]{2,1,0:T(8,128)(2,1)} %bitcast.3), calls=%async_computation.1 | async-start | bytes 786432 | tf_op jit(solution)/shard_map/all_to_all | solution.py:514
  62.8 6.0 %collective-permute-start.10 = (bf16[384,128]{1,0:T(8,128)(2,1)S(1)}, bf16[384,128]{1,0:T(8,128)(2,1)S(1)}, u32[]{:S(2)}, u32[]{:S(2)}) collective-permute-start(bf16[384,128]{1,0:T(8,128)(2,1)S(1)} %get-tuple-element.60), channel_id=1, source_target_pairs={{0,2},{1,3},{2,0},{3,1},{4,6},{5,7},{6,4},{7,5},{8,10},{9,11},{10,... | collective-permute-start | bytes 294920 | tf_op jit(solution)/shard_map/ppermute | solution.py:435
  64.9 6.6 %collective-permute-start.11 = (bf16[384,128]{1,0:T(8,128)(2,1)S(1)}, bf16[384,128]{1,0:T(8,128)(2,1)S(1)}, u32[]{:S(2)}, u32[]{:S(2)}) collective-permute-start(bf16[384,128]{1,0:T(8,128)(2,1)S(1)} %get-tuple-element.61), channel_id=1, source_target_pairs={{0,3},{1,2},{2,1},{3,0},{4,7},{5,6},{6,5},{7,4},{8,11},{9,10},{10,... | collective-permute-start | bytes 294920 | tf_op jit(solution)/shard_map/ppermute | solution.py:435
  64.9 6.6 %collective-permute-start.9 = (bf16[384,128]{1,0:T(8,128)(2,1)S(1)}, bf16[384,128]{1,0:T(8,128)(2,1)S(1)}, u32[]{:S(2)}, u32[]{:S(2)}) collective-permute-start(bf16[384,128]{1,0:T(8,128)(2,1)S(1)} %get-tuple-element.59), channel_id=1, source_target_pairs={{0,1},{1,0},{2,3},{3,2},{4,5},{5,4},{6,7},{7,6},{8,9},{9,8},{10,11... | collective-permute-start | bytes 294920 | tf_op jit(solution)/shard_map/ppermute | solution.py:435

commit v3 on v2

--- a/solution.py
+++ b/solution.py
@@ -448,6 +448,7 @@
             (idx, *packed, *linear),
             (((owners, rows, 2 * head), bf16),) + (msg,) * heads,
             [pltpu.VMEM(a.shape, a.dtype) for a in (*packed, *linear)] + [pltpu.SemaphoreType.DMA((9,))],
+            grant=58,
             space=HBM,
         )
     else:
@@ -457,6 +458,7 @@
             (idx, *linear),
             (msg,) * heads,
             [pltpu.VMEM(a.shape, a.dtype) for a in linear] + [pltpu.SemaphoreType.DMA((4,))],
+            grant=58,
             space=HBM,
         )
     own = lax.all_to_all(send, "zx", 0, 0, tiled=True)

time: 74 us -> 66.5 us (0.90)
  local copies, waits for them, and re-layouts: 7.62 us -> 0.03 us
    unnamed x20 -> x10, local copies, waits for them, and re-layouts: 7.62 us -> 0.03 us
where the time goes in v3:
time: 66.5 us; the launch traced here: 66.1 us
  waiting for transfers between devices  29.7 us (45%)
  starting transfers between devices  24.7 us (37%)
  Pallas kernels  10.1 us (15%)
  other arithmetic  0.83 us (1%)
  between operations  0.79 us (1%)
    ppermute x8, waiting for transfers between devices, swap(): return lax.ppermute(a, line, [(i, i ^ k) for i in range(n)])  17.8 us
    pallas_call x7, Pallas kernels, call(): pl.pallas_call(body, in_specs=in_specs, out_specs=tuple((VMEM for _ in ou...  10.1 us
    ppermute x4, starting transfers between devices, shift(): return lax.ppermute(a, line, pairs)  8.14 us
    all_to_all x1, starting transfers between devices, body(): own = lax.all_to_all(send, 'zx', 0, 0, tiled=True)  7.42 us
    all_to_all x1, waiting for transfers between devices, body(): own = lax.all_to_all(send, 'zx', 0, 0, tiled=True)  6.01 us
    ppermute x4, waiting for transfers between devices, shift(): return lax.ppermute(a, line, pairs)  5.39 us
    ppermute x8, starting transfers between devices, swap(): return lax.ppermute(a, line, [(i, i ^ k) for i in range(n)])  4.74 us
    all_to_all x1, starting transfers between devices, body(): parts = lax.all_to_all(parts, 'zx', 0, 0, tiled=True)  4.35 us
  transfers between devices with their start and end apart: 14, of which 8 were waited for; matrix products, arithmetic and copies ran while one was open for 0% of the time, Pallas kernels for 4%

profile of v3, /device:TPU:0, one launch (start us, length us, event | category | flops | bytes accessed | tf_op | source)
XLA Modules:
  0.0 66.1 jit_solution(7614785969234460760)
XLA Ops:
  0.6 2.7 %shard_map.137 = (bf16[8,168,256]{2,1,0:T(8,128)(2,1)}, bf16[400,128]{1,0:T(8,128)(2,1)}, bf16[400,128]{1,0:T(8,128)(2,1)}, bf16[400,128]{1,0:T(8,128)(2,1)}, bf16[400,128]{1,0:T(8,128)(2,1)}) custom-call(s32[1]{0:T(128)} %bitcast.idx_ref.refs_0_, bf16[128,512]{1,0:T(8,128)(2,1)} %refs_0_.1, bf16[128,128]{1,0:T(8,128)(2,1)} %refs_1_.1, ...), custom_call_target="tpu_custom_call" | custom-call | flops 1048576 | bytes 1048576 | tf_op jit(solution)/shard_map/pallas_call | solution.py:396
  3.4 7.4 %all-to-all-start = ((bf16[8,168,256]{2,1,0:T(8,128)(2,1)}), bf16[8,168,256]{2,1,0:T(8,128)(2,1)S(1)}, u32[]{:S(2)}, u32[]{:S(2)}) async-start(bf16[8,168,256]{2,1,0:T(8,128)(2,1)} %get-tuple-element.35), calls=%async_computation | async-start | bytes 1376256 | tf_op jit(solution)/shard_map/all_to_all | solution.py:464
  10.9 2.1 %collective-permute-start.1 = (bf16[400,128]{1,0:T(8,128)(2,1)S(1)}, bf16[400,128]{1,0:T(8,128)(2,1)S(1)}, u32[]{:S(2)}, u32[]{:S(2)}) collective-permute-start(bf16[400,128]{1,0:T(8,128)(2,1)S(1)} %copy-done.3), channel_id=1, source_target_pairs={{0,2},{1,3},{2,0},{3,1},{4,6},{5,7},{6,4},{7,5},{8,10},{9,11},{10,... | collective-permute-start | bytes 307208 | tf_op jit(solution)/shard_map/ppermute | solution.py:435
  13.1 9.3 %collective-permute-done.1.rest_2_ = bf16[400,128]{1,0:T(8,128)(2,1)S(1)} collective-permute-done((bf16[400,128]{1,0:T(8,128)(2,1)S(1)}, bf16[400,128]{1,0:T(8,128)(2,1)S(1)}, u32[]{:S(2)}, u32[]{:S(2)}) %collective-permute-start.1) | collective-permute-done | bytes 102432 | tf_op jit(solution)/shard_map/ppermute | solution.py:435
  22.4 0.4 shard_map.138
  22.8 6.0 %all-to-all-done.refs_2_ = bf16[8,168,256]{2,1,0:T(8,128)(2,1)S(1)} async-done(((bf16[8,168,256]{2,1,0:T(8,128)(2,1)}), bf16[8,168,256]{2,1,0:T(8,128)(2,1)S(1)}, u32[]{:S(2)}, u32[]{:S(2)}) %all-to-all-start) | async-done | bytes 688160 | tf_op jit(solution)/shard_map/all_to_all | solution.py:464
  28.8 2.1 %collective-permute-done.3.refs_3_ = bf16[8,168,256]{2,1,0:T(8,128)(2,1)S(1)} collective-permute-done((bf16[8,168,256]{2,1,0:T(8,128)(2,1)S(1)}, bf16[8,168,256]{2,1,0:T(8,128)(2,1)S(1)}, u32[]{:S(2)}, u32[]{:S(2)}) %collective-permute-start.3) | collective-permute-done | bytes 688160 | tf_op jit(solution)/shard_map/ppermute | solution.py:435
  30.9 4.1 %shard_map.139 = (f32[768,256]{1,0:T(8,128)S(1)}, bf16[768,256]{1,0:T(8,128)(2,1)S(1)}, bf16[512,128]{1,0:T(8,128)(2,1)S(1)}, f32[136,128]{1,0:T(8,128)S(1)}) custom-call(s32[1]{0:T(128)} %bitcast.idx_ref.refs_0_, s32[16,128]{1,0:T(8,128)S(1)} %bitcast.5, bf16[8,168,256]{2,1,0:T(8,128)(2,1)S(1)} %all-to-all-done.refs_2_, ...), custom_call_target="tpu_custom_call" | custom-call | flops 1073741824 | bytes 1048576 | tf_op jit(solution)/shard_map/pallas_call | solution.py:396
  35.2 2.4 %collective-permute-start.5 = (f32[136,128]{1,0:T(8,128)S(1)}, f32[136,128]{1,0:T(8,128)S(1)}, u32[]{:S(2)}, u32[]{:S(2)}) collective-permute-start(f32[136,128]{1,0:T(8,128)S(1)} %get-tuple-element.47), channel_id=1, source_target_pairs={{0,4},{1,5},{2,6},{3,7},{4,8},{5,9},{6,10},{7,11},{8,12},{9,13},{1... | collective-permute-start | bytes 208904 | tf_op jit(solution)/shard_map/ppermute | solution.py:439
  37.7 3.1 %collective-permute-start.6 = (f32[136,128]{1,0:T(8,128)S(1)}, f32[136,128]{1,0:T(8,128)S(1)}, u32[]{:S(2)}, u32[]{:S(2)}) collective-permute-start(f32[136,128]{1,0:T(8,128)S(1)} %get-tuple-element.47), channel_id=1, source_target_pairs={{0,8},{1,9},{2,10},{3,11},{4,12},{5,13},{6,14},{7,15},{16,24},{17,... | collective-permute-start | bytes 208904 | tf_op jit(solution)/shard_map/ppermute | solution.py:439
  40.8 1.3 %collective-permute-start.7 = (f32[136,128]{1,0:T(8,128)S(1)}, f32[136,128]{1,0:T(8,128)S(1)}, u32[]{:S(2)}, u32[]{:S(2)}) collective-permute-start(f32[136,128]{1,0:T(8,128)S(1)} %get-tuple-element.49), channel_id=1, source_target_pairs={{4,0},{5,1},{6,2},{7,3},{8,4},{9,5},{10,6},{11,7},{12,8},{13,9},{1... | collective-permute-start | bytes 208904 | tf_op jit(solution)/shard_map/ppermute | solution.py:439
  42.1 1.3 %collective-permute-start.8 = (f32[136,128]{1,0:T(8,128)S(1)}, f32[136,128]{1,0:T(8,128)S(1)}, u32[]{:S(2)}, u32[]{:S(2)}) collective-permute-start(f32[136,128]{1,0:T(8,128)S(1)} %get-tuple-element.49), channel_id=1, source_target_pairs={{8,0},{9,1},{10,2},{11,3},{12,4},{13,5},{14,6},{15,7},{24,16},{25,... | collective-permute-start | bytes 208904 | tf_op jit(solution)/shard_map/ppermute | solution.py:439
  43.4 1.1 %shard_map.140 = (bf16[512,128]{1,0:T(8,128)(2,1)S(1)}, f32[512,128]{1,0:T(8,128)S(1)}, f32[512,128]{1,0:T(8,128)S(1)}) custom-call(s32[1]{0:T(128)} %bitcast.idx_ref.refs_0_, s32[16,128]{1,0:T(8,128)S(1)} %bitcast.6, bf16[512,128]{1,0:T(8,128)(2,1)S(1)} %get-tuple-element.46.stream_ref, bf16[3,512,128]{2,1,0:T(8,128)(2,1)S(1)} %get-tuple-element.42.refs_4_.qkv, ...), custom_call_target="tpu_custom_call" | custom-call | flops 268435456 | bytes 1048576 | tf_op jit(solution)/shard_map/pallas_call | solution.py:396
  44.6 2.4 %collective-permute-done.7.rest_0_ = f32[136,128]{1,0:T(8,128)S(1)} collective-permute-done((f32[136,128]{1,0:T(8,128)S(1)}, f32[136,128]{1,0:T(8,128)S(1)}, u32[]{:S(2)}, u32[]{:S(2)}) %collective-permute-start.7) | collective-permute-done | bytes 69664 | tf_op jit(solution)/shard_map/ppermute | solution.py:439
  47.0 2.9 %collective-permute-done.8.rest_1_ = f32[136,128]{1,0:T(8,128)S(1)} collective-permute-done((f32[136,128]{1,0:T(8,128)S(1)}, f32[136,128]{1,0:T(8,128)S(1)}, u32[]{:S(2)}, u32[]{:S(2)}) %collective-permute-start.8) | collective-permute-done | bytes 69664 | tf_op jit(solution)/shard_map/ppermute | solution.py:439
  50.0 0.8 %add_convert_fusion = bf16[768,256]{1,0:T(8,128)(2,1)} fusion(f32[768,256]{1,0:T(8,128)S(1)} %get-tuple-element.44, bf16[768,256]{1,0:T(8,128)(2,1)S(1)} %collective-permute-done.4), kind=kLoop, calls=%fused_computation | loop fusion | flops 589824 | bytes 1572864 | tf_op jit(solution)/shard_map/convert_element_type | solution.py:515
  50.8 4.3 %all-to-all-start.1 = ((bf16[8,96,256]{2,1,0:T(8,128)(2,1)}), bf16[8,96,256]{2,1,0:T(8,128)(2,1)S(1)}, u32[]{:S(2)}, u32[]{:S(2)}) async-start(bf16[8,96,256]{2,1,0:T(8,128)(2,1)} %bitcast.3), calls=%async_computation.1 | async-start | bytes 786432 | tf_op jit(solution)/shard_map/all_to_all | solution.py:516
  55.1 0.4 shard_map.142
  55.5 2.1 %collective-permute-start.10 = (bf16[384,128]{1,0:T(8,128)(2,1)S(1)}, bf16[384,128]{1,0:T(8,128)(2,1)S(1)}, u32[]{:S(2)}, u32[]{:S(2)}) collective-permute-start(bf16[384,128]{1,0:T(8,128)(2,1)S(1)} %get-tuple-element.60), channel_id=1, source_target_pairs={{0,2},{1,3},{2,0},{3,1},{4,6},{5,7},{6,4},{7,5},{8,10},{9,11},{10,... | collective-permute-start | bytes 294920 | tf_op jit(solution)/shard_map/ppermute | solution.py:435
  57.8 3.7 %collective-permute-done.10.rest_2_ = bf16[384,128]{1,0:T(8,128)(2,1)S(1)} collective-permute-done((bf16[384,128]{1,0:T(8,128)(2,1)S(1)}, bf16[384,128]{1,0:T(8,128)(2,1)S(1)}, u32[]{:S(2)}, u32[]{:S(2)}) %collective-permute-start.10) | collective-permute-done | bytes 98336 | tf_op jit(solution)/shard_map/ppermute | solution.py:435
  61.5 2.7 %collective-permute-done.11.rest_3_ = bf16[384,128]{1,0:T(8,128)(2,1)S(1)} collective-permute-done((bf16[384,128]{1,0:T(8,128)(2,1)S(1)}, bf16[384,128]{1,0:T(8,128)(2,1)S(1)}, u32[]{:S(2)}, u32[]{:S(2)}) %collective-permute-start.11) | collective-permute-done | bytes 98336 | tf_op jit(solution)/shard_map/ppermute | solution.py:435
  64.2 0.8 %shard_map.143 = (bf16[128,512]{1,0:T(8,128)(2,1)}, bf16[128,512]{1,0:T(8,128)(2,1)}, bf16[128,512]{1,0:T(8,128)(2,1)}) custom-call(s32[1]{0:T(128)} %bitcast.idx_ref.refs_0_, bf16[384,128]{1,0:T(8,128)(2,1)S(1)} %get-tuple-element.58.rest_0_, bf16[384,128]{1,0:T(8,128)(2,1)S(1)} %collective-permute-done.9.rest_1_, ...), custom_call_target="tpu_custom_call" | custom-call | flops 1048576 | bytes 1048576 | tf_op jit(solution)/shard_map/pallas_call | solution.py:396
  65.0 0.5 all-to-all-done.1.parts
  65.5 0.7 %shard_map.141 = (bf16[128,128]{1,0:T(8,128)(2,1)}, bf16[128,128]{1,0:T(8,128)(2,1)}) custom-call(bf16[8,96,256]{2,1,0:T(8,128)(2,1)S(1)} %all-to-all-done.1.parts), custom_call_target="tpu_custom_call" | custom-call | flops 1048576 | bytes 1048576 | tf_op jit(solution)/shard_map/pallas_call | solution.py:396
  (22 shorter events, 0.6 us)
Async XLA Ops:
  3.3 7.5 %copy-start.4 = (bf16[400,128]{1,0:T(8,128)(2,1)S(1)}, bf16[400,128]{1,0:T(8,128)(2,1)}, u32[]{:S(2)}) copy-start(bf16[400,128]{1,0:T(8,128)(2,1)} %get-tuple-element.37) | copy-start | bytes 307204
  3.3 7.6 %copy-start.3 = (bf16[400,128]{1,0:T(8,128)(2,1)S(1)}, bf16[400,128]{1,0:T(8,128)(2,1)}, u32[]{:S(2)}) copy-start(bf16[400,128]{1,0:T(8,128)(2,1)} %get-tuple-element.38) | copy-start | bytes 307204
  3.3 9.6 %copy-start.2 = (bf16[400,128]{1,0:T(8,128)(2,1)S(1)}, bf16[400,128]{1,0:T(8,128)(2,1)}, u32[]{:S(2)}) copy-start(bf16[400,128]{1,0:T(8,128)(2,1)} %get-tuple-element.39) | copy-start | bytes 307204
  3.3 19.0 %copy-start = (bf16[400,128]{1,0:T(8,128)(2,1)S(1)}, bf16[400,128]{1,0:T(8,128)(2,1)}, u32[]{:S(2)}) copy-start(bf16[400,128]{1,0:T(8,128)(2,1)} %get-tuple-element.36.rest_0_) | copy-start | bytes 307204
  3.4 25.4 %all-to-all-start = ((bf16[8,168,256]{2,1,0:T(8,128)(2,1)}), bf16[8,168,256]{2,1,0:T(8,128)(2,1)S(1)}, u32[]{:S(2)}, u32[]{:S(2)}) async-start(bf16[8,168,256]{2,1,0:T(8,128)(2,1)} %get-tuple-element.35), calls=%async_computation | async-start | bytes 1376256 | tf_op jit(solution)/shard_map/all_to_all | solution.py:464
  10.8 11.6 %copy-start.1 = (s32[2048]{0:T(1024)S(1)}, s32[2048]{0:T(1024)}, u32[]{:S(2)}) copy-start(s32[2048]{0:T(1024)} %param.19) | copy-start | bytes 24580
  10.8 2.3 %collective-permute-start = (bf16[400,128]{1,0:T(8,128)(2,1)S(1)}, bf16[400,128]{1,0:T(8,128)(2,1)S(1)}, u32[]{:S(2)}, u32[]{:S(2)}) collective-permute-start(bf16[400,128]{1,0:T(8,128)(2,1)S(1)} %copy-done.4), channel_id=1, source_target_pairs={{0,1},{1,0},{2,3},{3,2},{4,5},{5,4},{6,7},{7,6},{8,9},{9,8},{10,11... | collective-permute-start | bytes 307208 | tf_op jit(solution)/shard_map/ppermute | solution.py:435
  10.9 11.5 %collective-permute-start.1 = (bf16[400,128]{1,0:T(8,128)(2,1)S(1)}, bf16[400,128]{1,0:T(8,128)(2,1)S(1)}, u32[]{:S(2)}, u32[]{:S(2)}) collective-permute-start(bf16[400,128]{1,0:T(8,128)(2,1)S(1)} %copy-done.3), channel_id=1, source_target_pairs={{0,2},{1,3},{2,0},{3,1},{4,6},{5,7},{6,4},{7,5},{8,10},{9,11},{10,... | collective-permute-start | bytes 307208 | tf_op jit(solution)/shard_map/ppermute | solution.py:435
  13.0 9.4 %collective-permute-start.2 = (bf16[400,128]{1,0:T(8,128)(2,1)S(1)}, bf16[400,128]{1,0:T(8,128)(2,1)S(1)}, u32[]{:S(2)}, u32[]{:S(2)}) collective-permute-start(bf16[400,128]{1,0:T(8,128)(2,1)S(1)} %copy-done.2), channel_id=1, source_target_pairs={{0,3},{1,2},{2,1},{3,0},{4,7},{5,6},{6,5},{7,4},{8,11},{9,10},{10,... | collective-permute-start | bytes 307208 | tf_op jit(solution)/shard_map/ppermute | solution.py:435
  28.8 2.1 %collective-permute-start.3 = (bf16[8,168,256]{2,1,0:T(8,128)(2,1)S(1)}, bf16[8,168,256]{2,1,0:T(8,128)(2,1)S(1)}, u32[]{:S(2)}, u32[]{:S(2)}) collective-permute-start(bf16[8,168,256]{2,1,0:T(8,128)(2,1)S(1)} %all-to-all-done.refs_2_), channel_id=1, source_target_pairs={{0,1},{1,0},{2,3},{3,2},{4,5},{5,4},{6,7},{7,6},{8,9},{9,8},{10,11... | collective-permute-start | bytes 2064392 | tf_op jit(solution)/shard_map/ppermute | solution.py:435
  35.0 14.9 %collective-permute-start.4 = (bf16[768,256]{1,0:T(8,128)(2,1)S(1)}, bf16[768,256]{1,0:T(8,128)(2,1)S(1)}, u32[]{:S(2)}, u32[]{:S(2)}) collective-permute-start(bf16[768,256]{1,0:T(8,128)(2,1)S(1)} %get-tuple-element.45), channel_id=1, source_target_pairs={{0,1},{1,0},{2,3},{3,2},{4,5},{5,4},{6,7},{7,6},{8,9},{9,8},{10,11... | collective-permute-start | bytes 1179656 | tf_op jit(solution)/shard_map/ppermute | solution.py:435
  35.2 8.2 %collective-permute-start.5 = (f32[136,128]{1,0:T(8,128)S(1)}, f32[136,128]{1,0:T(8,128)S(1)}, u32[]{:S(2)}, u32[]{:S(2)}) collective-permute-start(f32[136,128]{1,0:T(8,128)S(1)} %get-tuple-element.47), channel_id=1, source_target_pairs={{0,4},{1,5},{2,6},{3,7},{4,8},{5,9},{6,10},{7,11},{8,12},{9,13},{1... | collective-permute-start | bytes 208904 | tf_op jit(solution)/shard_map/ppermute | solution.py:439
  37.7 5.7 %collective-permute-start.6 = (f32[136,128]{1,0:T(8,128)S(1)}, f32[136,128]{1,0:T(8,128)S(1)}, u32[]{:S(2)}, u32[]{:S(2)}) collective-permute-start(f32[136,128]{1,0:T(8,128)S(1)} %get-tuple-element.47), channel_id=1, source_target_pairs={{0,8},{1,9},{2,10},{3,11},{4,12},{5,13},{6,14},{7,15},{16,24},{17,... | collective-permute-start | bytes 208904 | tf_op jit(solution)/shard_map/ppermute | solution.py:439
  40.8 6.2 %collective-permute-start.7 = (f32[136,128]{1,0:T(8,128)S(1)}, f32[136,128]{1,0:T(8,128)S(1)}, u32[]{:S(2)}, u32[]{:S(2)}) collective-permute-start(f32[136,128]{1,0:T(8,128)S(1)} %get-tuple-element.49), channel_id=1, source_target_pairs={{4,0},{5,1},{6,2},{7,3},{8,4},{9,5},{10,6},{11,7},{12,8},{13,9},{1... | collective-permute-start | bytes 208904 | tf_op jit(solution)/shard_map/ppermute | solution.py:439
  42.1 7.8 %collective-permute-start.8 = (f32[136,128]{1,0:T(8,128)S(1)}, f32[136,128]{1,0:T(8,128)S(1)}, u32[]{:S(2)}, u32[]{:S(2)}) collective-permute-start(f32[136,128]{1,0:T(8,128)S(1)} %get-tuple-element.49), channel_id=1, source_target_pairs={{8,0},{9,1},{10,2},{11,3},{12,4},{13,5},{14,6},{15,7},{24,16},{25,... | collective-permute-start | bytes 208904 | tf_op jit(solution)/shard_map/ppermute | solution.py:439
  50.8 14.7 %all-to-all-start.1 = ((bf16[8,96,256]{2,1,0:T(8,128)(2,1)}), bf16[8,96,256]{2,1,0:T(8,128)(2,1)S(1)}, u32[]{:S(2)}, u32[]{:S(2)}) async-start(bf16[8,96,256]{2,1,0:T(8,128)(2,1)} %bitcast.3), calls=%async_computation.1 | async-start | bytes 786432 | tf_op jit(solution)/shard_map/all_to_all | solution.py:516
  55.5 6.0 %collective-permute-start.10 = (bf16[384,128]{1,0:T(8,128)(2,1)S(1)}, bf16[384,128]{1,0:T(8,128)(2,1)S(1)}, u32[]{:S(2)}, u32[]{:S(2)}) collective-permute-start(bf16[384,128]{1,0:T(8,128)(2,1)S(1)} %get-tuple-element.60), channel_id=1, source_target_pairs={{0,2},{1,3},{2,0},{3,1},{4,6},{5,7},{6,4},{7,5},{8,10},{9,11},{10,... | collective-permute-start | bytes 294920 | tf_op jit(solution)/shard_map/ppermute | solution.py:435
  57.6 6.6 %collective-permute-start.11 = (bf16[384,128]{1,0:T(8,128)(2,1)S(1)}, bf16[384,128]{1,0:T(8,128)(2,1)S(1)}, u32[]{:S(2)}, u32[]{:S(2)}) collective-permute-start(bf16[384,128]{1,0:T(8,128)(2,1)S(1)} %get-tuple-element.61), channel_id=1, source_target_pairs={{0,3},{1,2},{2,1},{3,0},{4,7},{5,6},{6,5},{7,4},{8,11},{9,10},{10,... | collective-permute-start | bytes 294920 | tf_op jit(solution)/shard_map/ppermute | solution.py:435
  57.6 6.6 %collective-permute-start.9 = (bf16[384,128]{1,0:T(8,128)(2,1)S(1)}, bf16[384,128]{1,0:T(8,128)(2,1)S(1)}, u32[]{:S(2)}, u32[]{:S(2)}) collective-permute-start(bf16[384,128]{1,0:T(8,128)(2,1)S(1)} %get-tuple-element.59), channel_id=1, source_target_pairs={{0,1},{1,0},{2,3},{3,2},{4,5},{5,4},{6,7},{7,6},{8,9},{9,8},{10,11... | collective-permute-start | bytes 294920 | tf_op jit(solution)/shard_map/ppermute | solution.py:435

commit v4 on v3

--- a/solution.py
+++ b/solution.py
@@ -305,7 +305,7 @@
         out[:, head : 2 * head] = nn(p_scr[rows, :], grad).astype(out.dtype)
 
 
-def joined(states, g, span, bounds, step):
+def joined(states, g, span, bounds, step, positions):
     head = states[0].shape[1]
     one = jnp.zeros((1, 1), i32)
     total, passed = None, jnp.zeros((1, 1), f32)
@@ -313,7 +313,8 @@
         if step < 0:
             open_ = start_of(one + (g * span - 1), bounds) < (g - k + 1) * span
         else:
-            open_ = start_of(one + ((g + k) * span - 1), bounds) < (g + 1) * span
+            limit = jnp.where((g + k) * span < positions, (g + 1) * span, 0)
+            open_ = start_of(one + ((g + k) * span - 1), bounds) < limit
         part = ref[0:head, :] * jnp.where(open_, jnp.exp(passed), 0.0)
         total = part if total is None else total + part
         passed = passed + ref[head : head + 1, 0:1]
@@ -325,7 +326,7 @@
     span, head = stream_ref.shape
     g = lax.div(idx_ref[0], heads)
     bounds = run_starts(docs_ref[...])
-    earlier = joined(states, g, span, bounds, -1)
+    earlier = joined(states, g, span, bounds, -1, docs_ref.size)
     c_row, c_col = sums(dec[0:1, :])
     stream, query, key, value = stream_ref[...], qkv[0], qkv[1], qkv[2]
     t = iota((1, span), 1)
@@ -351,7 +352,7 @@
     tok = span // heads
     p, g = lax.rem(idx_ref[0], heads), lax.div(idx_ref[0], heads)
     bounds = run_starts(docs_ref[...])
-    later = joined(states, g, span, bounds, 1).astype(bf16)
+    later = joined(states, g, span, bounds, 1, docs_ref.size).astype(bf16)
     _, c_col = sums(dec[0:1, :])
     total = jnp.sum(dec[0:1, :], axis=1, keepdims=True)
     pos = g * span + iota((span, 1), 0)
@@ -434,8 +435,12 @@
     def swap(a, k):
         return lax.ppermute(a, line, [(i, i ^ k) for i in range(n)])
 
-    def shift(a, k):
-        pairs = [(i, i + k * heads) for i in range(n) if 0 <= i + k * heads < n]
+    def ring(a, k):
+        pairs = []
+        for i in range(n):
+            to = i // heads + k
+            if (k if to < planes else planes - k) < window:
+                pairs.append((i, (i + k * heads) % n))
         return lax.ppermute(a, line, pairs)
 
     msg = ((3 * tok + DEC_ROWS, head), bf16)
@@ -471,7 +476,6 @@
         (((3, span, head), bf16), ((8, span), f32), state),
     )
     own, forward = lax.optimization_barrier((own, forward))
-    before = [shift(forward, k) for k in range(1, window)]
     other = swap(own, 1)
 
     if aligned:
@@ -501,7 +505,9 @@
         grant=24 if aligned else 58,
     )
     taken = swap(give, 1)
-    after = [shift(backward, -k) for k in range(1, window)]
+    quarter = me // heads
+    rings = [ring(jnp.where(quarter + k < planes, forward, backward), k) for k in range(1, planes)]
+    before, after = rings[: window - 1], rings[::-1][: window - 1]
     square = [pltpu.VMEM((span, span), bf16)] * 2
     q_cot, k_part, v_part = call(
         functools.partial(linear_kernel, heads),

time: 66.5 us -> 63.1 us (0.949)
  starting transfers between devices: 24.7 us -> 20.5 us
  waiting for transfers between devices: 29.7 us -> 30.4 us
    ppermute x4 -> x3, starting transfers between devices: 8.14 us -> 5 us  [ring(): return lax.ppermute(a, line, pairs)]
    ppermute x8, waiting for transfers between devices: 17.8 us -> 20.2 us  [swap(): return lax.ppermute(a, line, [(i, i ^ k) for i in range(n)])]
    ppermute x4 -> x3, waiting for transfers between devices: 5.39 us -> 4.15 us  [ring(): return lax.ppermute(a, line, pairs)]
    all_to_all x1, starting transfers between devices: 4.35 us -> 3.45 us  [body(): parts = lax.all_to_all(parts, 'zx', 0, 0, tiled=True)]
  transfers between devices with their start and end apart: 14 -> 13, of which waited for: 8 -> 7; matrix products, arithmetic and copies ran while one was open for 0% -> 0% of each run, Pallas kernels for 4% -> 4%
where the time goes in v4:
time: 63.1 us; the launch traced here: 62.7 us
  waiting for transfers between devices  30.4 us (48%)
  starting transfers between devices  20.5 us (32%)
  Pallas kernels  10.1 us (16%)
  other arithmetic  0.91 us (1%)
  between operations  0.78 us (1%)
    ppermute x8, waiting for transfers between devices, swap(): return lax.ppermute(a, line, [(i, i ^ k) for i in range(n)])  20.2 us
    pallas_call x7, Pallas kernels, call(): pl.pallas_call(body, in_specs=in_specs, out_specs=tuple((VMEM for _ in ou...  10.1 us
    all_to_all x1, starting transfers between devices, body(): own = lax.all_to_all(send, 'zx', 0, 0, tiled=True)  7.42 us
    all_to_all x1, waiting for transfers between devices, body(): own = lax.all_to_all(send, 'zx', 0, 0, tiled=True)  6 us
    ppermute x3, starting transfers between devices, ring(): return lax.ppermute(a, line, pairs)  5 us
    ppermute x8, starting transfers between devices, swap(): return lax.ppermute(a, line, [(i, i ^ k) for i in range(n)])  4.65 us
    ppermute x3, waiting for transfers between devices, ring(): return lax.ppermute(a, line, pairs)  4.15 us
    all_to_all x1, starting transfers between devices, body(): parts = lax.all_to_all(parts, 'zx', 0, 0, tiled=True)  3.45 us
  transfers between devices with their start and end apart: 13, of which 7 were waited for; matrix products, arithmetic and copies ran while one was open for 0% of the time, Pallas kernels for 4%

profile of v4, /device:TPU:0, one launch (start us, length us, event | category | flops | bytes accessed | tf_op | source)
XLA Modules:
  0.0 62.7 jit_solution(5476547356389268594)
XLA Ops:
  0.6 2.7 %shard_map.137 = (bf16[8,168,256]{2,1,0:T(8,128)(2,1)}, bf16[400,128]{1,0:T(8,128)(2,1)}, bf16[400,128]{1,0:T(8,128)(2,1)}, bf16[400,128]{1,0:T(8,128)(2,1)}, bf16[400,128]{1,0:T(8,128)(2,1)}) custom-call(s32[1]{0:T(128)} %bitcast.idx_ref.refs_0_, bf16[128,512]{1,0:T(8,128)(2,1)} %refs_0_.1, bf16[128,128]{1,0:T(8,128)(2,1)} %refs_1_.1, ...), custom_call_target="tpu_custom_call" | custom-call | flops 1048576 | bytes 1048576 | tf_op jit(solution)/shard_map/pallas_call | solution.py:397
  3.4 7.4 %all-to-all-start = ((bf16[8,168,256]{2,1,0:T(8,128)(2,1)}), bf16[8,168,256]{2,1,0:T(8,128)(2,1)S(1)}, u32[]{:S(2)}, u32[]{:S(2)}) async-start(bf16[8,168,256]{2,1,0:T(8,128)(2,1)} %get-tuple-element.35), calls=%async_computation | async-start | bytes 1376256 | tf_op jit(solution)/shard_map/all_to_all | solution.py:469
  10.9 2.1 %collective-permute-start.1 = (bf16[400,128]{1,0:T(8,128)(2,1)S(1)}, bf16[400,128]{1,0:T(8,128)(2,1)S(1)}, u32[]{:S(2)}, u32[]{:S(2)}) collective-permute-start(bf16[400,128]{1,0:T(8,128)(2,1)S(1)} %copy-done.3), channel_id=1, source_target_pairs={{0,2},{1,3},{2,0},{3,1},{4,6},{5,7},{6,4},{7,5},{8,10},{9,11},{10,... | collective-permute-start | bytes 307208 | tf_op jit(solution)/shard_map/ppermute | solution.py:436
  13.1 9.3 %collective-permute-done.1.rest_2_ = bf16[400,128]{1,0:T(8,128)(2,1)S(1)} collective-permute-done((bf16[400,128]{1,0:T(8,128)(2,1)S(1)}, bf16[400,128]{1,0:T(8,128)(2,1)S(1)}, u32[]{:S(2)}, u32[]{:S(2)}) %collective-permute-start.1) | collective-permute-done | bytes 102432 | tf_op jit(solution)/shard_map/ppermute | solution.py:436
  22.4 0.4 shard_map.138
  22.8 6.0 %all-to-all-done.refs_2_ = bf16[8,168,256]{2,1,0:T(8,128)(2,1)S(1)} async-done(((bf16[8,168,256]{2,1,0:T(8,128)(2,1)}), bf16[8,168,256]{2,1,0:T(8,128)(2,1)S(1)}, u32[]{:S(2)}, u32[]{:S(2)}) %all-to-all-start) | async-done | bytes 688160 | tf_op jit(solution)/shard_map/all_to_all | solution.py:469
  28.8 2.1 %collective-permute-done.3.refs_3_ = bf16[8,168,256]{2,1,0:T(8,128)(2,1)S(1)} collective-permute-done((bf16[8,168,256]{2,1,0:T(8,128)(2,1)S(1)}, bf16[8,168,256]{2,1,0:T(8,128)(2,1)S(1)}, u32[]{:S(2)}, u32[]{:S(2)}) %collective-permute-start.3) | collective-permute-done | bytes 688160 | tf_op jit(solution)/shard_map/ppermute | solution.py:436
  30.9 4.1 %shard_map.139 = (f32[768,256]{1,0:T(8,128)S(1)}, bf16[768,256]{1,0:T(8,128)(2,1)S(1)}, bf16[512,128]{1,0:T(8,128)(2,1)S(1)}, f32[136,128]{1,0:T(8,128)S(1)}) custom-call(s32[1]{0:T(128)} %bitcast.idx_ref.refs_0_, s32[16,128]{1,0:T(8,128)S(1)} %bitcast.5, bf16[8,168,256]{2,1,0:T(8,128)(2,1)S(1)} %all-to-all-done.refs_2_, ...), custom_call_target="tpu_custom_call" | custom-call | flops 1073741824 | bytes 1048576 | tf_op jit(solution)/shard_map/pallas_call | solution.py:397
  35.0 0.2 collective-permute-start.4
  35.2 2.4 %collective-permute-start.5 = (f32[136,128]{1,0:T(8,128)S(1)}, f32[136,128]{1,0:T(8,128)S(1)}, u32[]{:S(2)}, u32[]{:S(2)}) collective-permute-start(f32[136,128]{1,0:T(8,128)S(1)} %get-tuple-element.67), channel_id=1, source_target_pairs={{0,4},{1,5},{2,6},{3,7},{4,8},{5,9},{6,10},{7,11},{8,12},{9,13},{1... | collective-permute-start | bytes 208904 | tf_op jit(solution)/shard_map/ppermute | solution.py:444
  37.7 1.3 %collective-permute-start.6 = (f32[136,128]{1,0:T(8,128)S(1)}, f32[136,128]{1,0:T(8,128)S(1)}, u32[]{:S(2)}, u32[]{:S(2)}) collective-permute-start(f32[136,128]{1,0:T(8,128)S(1)} %get-tuple-element.66), channel_id=1, source_target_pairs={{0,8},{1,9},{2,10},{3,11},{4,12},{5,13},{6,14},{7,15},{8,0},{9,1},... | collective-permute-start | bytes 208904 | tf_op jit(solution)/shard_map/ppermute | solution.py:444
  39.0 1.3 %collective-permute-start.7 = (f32[136,128]{1,0:T(8,128)S(1)}, f32[136,128]{1,0:T(8,128)S(1)}, u32[]{:S(2)}, u32[]{:S(2)}) collective-permute-start(f32[136,128]{1,0:T(8,128)S(1)} %get-tuple-element.65), channel_id=1, source_target_pairs={{4,0},{5,1},{6,2},{7,3},{8,4},{9,5},{10,6},{11,7},{12,8},{13,9},{1... | collective-permute-start | bytes 208904 | tf_op jit(solution)/shard_map/ppermute | solution.py:444
  40.3 3.9 %collective-permute-done.6.rest_1_ = f32[136,128]{1,0:T(8,128)S(1)} collective-permute-done((f32[136,128]{1,0:T(8,128)S(1)}, f32[136,128]{1,0:T(8,128)S(1)}, u32[]{:S(2)}, u32[]{:S(2)}) %collective-permute-start.6) | collective-permute-done | bytes 69664 | tf_op jit(solution)/shard_map/ppermute | solution.py:444
  44.1 1.1 %shard_map.140 = (bf16[512,128]{1,0:T(8,128)(2,1)S(1)}, f32[512,128]{1,0:T(8,128)S(1)}, f32[512,128]{1,0:T(8,128)S(1)}) custom-call(s32[1]{0:T(128)} %bitcast.idx_ref.refs_0_, s32[16,128]{1,0:T(8,128)S(1)} %bitcast.6, bf16[512,128]{1,0:T(8,128)(2,1)S(1)} %get-tuple-element.46.stream_ref, bf16[3,512,128]{2,1,0:T(8,128)(2,1)S(1)} %get-tuple-element.42.refs_4_.qkv, ...), custom_call_target="tpu_custom_call" | custom-call | flops 268435456 | bytes 1048576 | tf_op jit(solution)/shard_map/pallas_call | solution.py:397
  45.3 0.3 collective-permute-done.7.rest_0_
  45.6 0.9 %add_convert_fusion = bf16[768,256]{1,0:T(8,128)(2,1)} fusion(f32[768,256]{1,0:T(8,128)S(1)} %get-tuple-element.44, bf16[768,256]{1,0:T(8,128)(2,1)S(1)} %collective-permute-done.4), kind=kLoop, calls=%fused_computation | loop fusion | flops 589824 | bytes 1572864 | tf_op jit(solution)/shard_map/convert_element_type | solution.py:521
  46.4 3.5 %all-to-all-start.1 = ((bf16[8,96,256]{2,1,0:T(8,128)(2,1)}), bf16[8,96,256]{2,1,0:T(8,128)(2,1)S(1)}, u32[]{:S(2)}, u32[]{:S(2)}) async-start(bf16[8,96,256]{2,1,0:T(8,128)(2,1)} %bitcast.3), calls=%async_computation.1 | async-start | bytes 786432 | tf_op jit(solution)/shard_map/all_to_all | solution.py:522
  49.9 0.4 shard_map.142
  50.3 1.1 %collective-permute-start.10 = (bf16[384,128]{1,0:T(8,128)(2,1)S(1)}, bf16[384,128]{1,0:T(8,128)(2,1)S(1)}, u32[]{:S(2)}, u32[]{:S(2)}) collective-permute-start(bf16[384,128]{1,0:T(8,128)(2,1)S(1)} %get-tuple-element.61), channel_id=1, source_target_pairs={{0,3},{1,2},{2,1},{3,0},{4,7},{5,6},{6,5},{7,4},{8,11},{9,10},{10,... | collective-permute-start | bytes 294920 | tf_op jit(solution)/shard_map/ppermute | solution.py:436
  51.3 1.0 %collective-permute-start.8 = (bf16[384,128]{1,0:T(8,128)(2,1)S(1)}, bf16[384,128]{1,0:T(8,128)(2,1)S(1)}, u32[]{:S(2)}, u32[]{:S(2)}) collective-permute-start(bf16[384,128]{1,0:T(8,128)(2,1)S(1)} %get-tuple-element.59), channel_id=1, source_target_pairs={{0,1},{1,0},{2,3},{3,2},{4,5},{5,4},{6,7},{7,6},{8,9},{9,8},{10,11... | collective-permute-start | bytes 294920 | tf_op jit(solution)/shard_map/ppermute | solution.py:436
  52.5 4.5 %collective-permute-done.10.rest_3_ = bf16[384,128]{1,0:T(8,128)(2,1)S(1)} collective-permute-done((bf16[384,128]{1,0:T(8,128)(2,1)S(1)}, bf16[384,128]{1,0:T(8,128)(2,1)S(1)}, u32[]{:S(2)}, u32[]{:S(2)}) %collective-permute-start.10) | collective-permute-done | bytes 98336 | tf_op jit(solution)/shard_map/ppermute | solution.py:436
  57.0 4.2 %collective-permute-done.9.rest_2_ = bf16[384,128]{1,0:T(8,128)(2,1)S(1)} collective-permute-done((bf16[384,128]{1,0:T(8,128)(2,1)S(1)}, bf16[384,128]{1,0:T(8,128)(2,1)S(1)}, u32[]{:S(2)}, u32[]{:S(2)}) %collective-permute-start.9) | collective-permute-done | bytes 98336 | tf_op jit(solution)/shard_map/ppermute | solution.py:436
  61.2 0.8 %shard_map.143 = (bf16[128,512]{1,0:T(8,128)(2,1)}, bf16[128,512]{1,0:T(8,128)(2,1)}, bf16[128,512]{1,0:T(8,128)(2,1)}) custom-call(s32[1]{0:T(128)} %bitcast.idx_ref.refs_0_, bf16[384,128]{1,0:T(8,128)(2,1)S(1)} %get-tuple-element.58.rest_0_, bf16[384,128]{1,0:T(8,128)(2,1)S(1)} %collective-permute-done.8.rest_1_, ...), custom_call_target="tpu_custom_call" | custom-call | flops 1048576 | bytes 1048576 | tf_op jit(solution)/shard_map/pallas_call | solution.py:397
  62.0 0.7 %shard_map.141 = (bf16[128,128]{1,0:T(8,128)(2,1)}, bf16[128,128]{1,0:T(8,128)(2,1)}) custom-call(bf16[8,96,256]{2,1,0:T(8,128)(2,1)S(1)} %all-to-all-done.1.parts), custom_call_target="tpu_custom_call" | custom-call | flops 1048576 | bytes 1048576 | tf_op jit(solution)/shard_map/pallas_call | solution.py:397
  (21 shorter events, 0.4 us)
Async XLA Ops:
  3.3 7.5 %copy-start.4 = (bf16[400,128]{1,0:T(8,128)(2,1)S(1)}, bf16[400,128]{1,0:T(8,128)(2,1)}, u32[]{:S(2)}) copy-start(bf16[400,128]{1,0:T(8,128)(2,1)} %get-tuple-element.37) | copy-start | bytes 307204
  3.3 7.6 %copy-start.3 = (bf16[400,128]{1,0:T(8,128)(2,1)S(1)}, bf16[400,128]{1,0:T(8,128)(2,1)}, u32[]{:S(2)}) copy-start(bf16[400,128]{1,0:T(8,128)(2,1)} %get-tuple-element.38) | copy-start | bytes 307204
  3.3 9.6 %copy-start.2 = (bf16[400,128]{1,0:T(8,128)(2,1)S(1)}, bf16[400,128]{1,0:T(8,128)(2,1)}, u32[]{:S(2)}) copy-start(bf16[400,128]{1,0:T(8,128)(2,1)} %get-tuple-element.39) | copy-start | bytes 307204
  3.3 19.0 %copy-start = (bf16[400,128]{1,0:T(8,128)(2,1)S(1)}, bf16[400,128]{1,0:T(8,128)(2,1)}, u32[]{:S(2)}) copy-start(bf16[400,128]{1,0:T(8,128)(2,1)} %get-tuple-element.36.rest_0_) | copy-start | bytes 307204
  3.4 25.4 %all-to-all-start = ((bf16[8,168,256]{2,1,0:T(8,128)(2,1)}), bf16[8,168,256]{2,1,0:T(8,128)(2,1)S(1)}, u32[]{:S(2)}, u32[]{:S(2)}) async-start(bf16[8,168,256]{2,1,0:T(8,128)(2,1)} %get-tuple-element.35), calls=%async_computation | async-start | bytes 1376256 | tf_op jit(solution)/shard_map/all_to_all | solution.py:469
  10.8 11.6 %copy-start.1 = (s32[2048]{0:T(1024)S(1)}, s32[2048]{0:T(1024)}, u32[]{:S(2)}) copy-start(s32[2048]{0:T(1024)} %param.19) | copy-start | bytes 24580
  10.8 2.3 %collective-permute-start = (bf16[400,128]{1,0:T(8,128)(2,1)S(1)}, bf16[400,128]{1,0:T(8,128)(2,1)S(1)}, u32[]{:S(2)}, u32[]{:S(2)}) collective-permute-start(bf16[400,128]{1,0:T(8,128)(2,1)S(1)} %copy-done.4), channel_id=1, source_target_pairs={{0,1},{1,0},{2,3},{3,2},{4,5},{5,4},{6,7},{7,6},{8,9},{9,8},{10,11... | collective-permute-start | bytes 307208 | tf_op jit(solution)/shard_map/ppermute | solution.py:436
  10.9 11.5 %collective-permute-start.1 = (bf16[400,128]{1,0:T(8,128)(2,1)S(1)}, bf16[400,128]{1,0:T(8,128)(2,1)S(1)}, u32[]{:S(2)}, u32[]{:S(2)}) collective-permute-start(bf16[400,128]{1,0:T(8,128)(2,1)S(1)} %copy-done.3), channel_id=1, source_target_pairs={{0,2},{1,3},{2,0},{3,1},{4,6},{5,7},{6,4},{7,5},{8,10},{9,11},{10,... | collective-permute-start | bytes 307208 | tf_op jit(solution)/shard_map/ppermute | solution.py:436
  13.0 9.4 %collective-permute-start.2 = (bf16[400,128]{1,0:T(8,128)(2,1)S(1)}, bf16[400,128]{1,0:T(8,128)(2,1)S(1)}, u32[]{:S(2)}, u32[]{:S(2)}) collective-permute-start(bf16[400,128]{1,0:T(8,128)(2,1)S(1)} %copy-done.2), channel_id=1, source_target_pairs={{0,3},{1,2},{2,1},{3,0},{4,7},{5,6},{6,5},{7,4},{8,11},{9,10},{10,... | collective-permute-start | bytes 307208 | tf_op jit(solution)/shard_map/ppermute | solution.py:436
  28.8 2.1 %collective-permute-start.3 = (bf16[8,168,256]{2,1,0:T(8,128)(2,1)S(1)}, bf16[8,168,256]{2,1,0:T(8,128)(2,1)S(1)}, u32[]{:S(2)}, u32[]{:S(2)}) collective-permute-start(bf16[8,168,256]{2,1,0:T(8,128)(2,1)S(1)} %all-to-all-done.refs_2_), channel_id=1, source_target_pairs={{0,1},{1,0},{2,3},{3,2},{4,5},{5,4},{6,7},{7,6},{8,9},{9,8},{10,11... | collective-permute-start | bytes 2064392 | tf_op jit(solution)/shard_map/ppermute | solution.py:436
  35.0 10.5 %collective-permute-start.4 = (bf16[768,256]{1,0:T(8,128)(2,1)S(1)}, bf16[768,256]{1,0:T(8,128)(2,1)S(1)}, u32[]{:S(2)}, u32[]{:S(2)}) collective-permute-start(bf16[768,256]{1,0:T(8,128)(2,1)S(1)} %get-tuple-element.45), channel_id=1, source_target_pairs={{0,1},{1,0},{2,3},{3,2},{4,5},{5,4},{6,7},{7,6},{8,9},{9,8},{10,11... | collective-permute-start | bytes 1179656 | tf_op jit(solution)/shard_map/ppermute | solution.py:436
  35.2 5.0 %collective-permute-start.5 = (f32[136,128]{1,0:T(8,128)S(1)}, f32[136,128]{1,0:T(8,128)S(1)}, u32[]{:S(2)}, u32[]{:S(2)}) collective-permute-start(f32[136,128]{1,0:T(8,128)S(1)} %get-tuple-element.67), channel_id=1, source_target_pairs={{0,4},{1,5},{2,6},{3,7},{4,8},{5,9},{6,10},{7,11},{8,12},{9,13},{1... | collective-permute-start | bytes 208904 | tf_op jit(solution)/shard_map/ppermute | solution.py:444
  37.7 6.4 %collective-permute-start.6 = (f32[136,128]{1,0:T(8,128)S(1)}, f32[136,128]{1,0:T(8,128)S(1)}, u32[]{:S(2)}, u32[]{:S(2)}) collective-permute-start(f32[136,128]{1,0:T(8,128)S(1)} %get-tuple-element.66), channel_id=1, source_target_pairs={{0,8},{1,9},{2,10},{3,11},{4,12},{5,13},{6,14},{7,15},{8,0},{9,1},... | collective-permute-start | bytes 208904 | tf_op jit(solution)/shard_map/ppermute | solution.py:444
  39.0 6.6 %collective-permute-start.7 = (f32[136,128]{1,0:T(8,128)S(1)}, f32[136,128]{1,0:T(8,128)S(1)}, u32[]{:S(2)}, u32[]{:S(2)}) collective-permute-start(f32[136,128]{1,0:T(8,128)S(1)} %get-tuple-element.65), channel_id=1, source_target_pairs={{4,0},{5,1},{6,2},{7,3},{8,4},{9,5},{10,6},{11,7},{12,8},{13,9},{1... | collective-permute-start | bytes 208904 | tf_op jit(solution)/shard_map/ppermute | solution.py:444
  46.4 15.6 %all-to-all-start.1 = ((bf16[8,96,256]{2,1,0:T(8,128)(2,1)}), bf16[8,96,256]{2,1,0:T(8,128)(2,1)S(1)}, u32[]{:S(2)}, u32[]{:S(2)}) async-start(bf16[8,96,256]{2,1,0:T(8,128)(2,1)} %bitcast.3), calls=%async_computation.1 | async-start | bytes 786432 | tf_op jit(solution)/shard_map/all_to_all | solution.py:522
  50.3 6.7 %collective-permute-start.10 = (bf16[384,128]{1,0:T(8,128)(2,1)S(1)}, bf16[384,128]{1,0:T(8,128)(2,1)S(1)}, u32[]{:S(2)}, u32[]{:S(2)}) collective-permute-start(bf16[384,128]{1,0:T(8,128)(2,1)S(1)} %get-tuple-element.61), channel_id=1, source_target_pairs={{0,3},{1,2},{2,1},{3,0},{4,7},{5,6},{6,5},{7,4},{8,11},{9,10},{10,... | collective-permute-start | bytes 294920 | tf_op jit(solution)/shard_map/ppermute | solution.py:436
  51.3 5.7 %collective-permute-start.8 = (bf16[384,128]{1,0:T(8,128)(2,1)S(1)}, bf16[384,128]{1,0:T(8,128)(2,1)S(1)}, u32[]{:S(2)}, u32[]{:S(2)}) collective-permute-start(bf16[384,128]{1,0:T(8,128)(2,1)S(1)} %get-tuple-element.59), channel_id=1, source_target_pairs={{0,1},{1,0},{2,3},{3,2},{4,5},{5,4},{6,7},{7,6},{8,9},{9,8},{10,11... | collective-permute-start | bytes 294920 | tf_op jit(solution)/shard_map/ppermute | solution.py:436
  52.4 8.9 %collective-permute-start.9 = (bf16[384,128]{1,0:T(8,128)(2,1)S(1)}, bf16[384,128]{1,0:T(8,128)(2,1)S(1)}, u32[]{:S(2)}, u32[]{:S(2)}) collective-permute-start(bf16[384,128]{1,0:T(8,128)(2,1)S(1)} %get-tuple-element.60), channel_id=1, source_target_pairs={{0,2},{1,3},{2,0},{3,1},{4,6},{5,7},{6,4},{7,5},{8,10},{9,11},{10,... | collective-permute-start | bytes 294920 | tf_op jit(solution)/shard_map/ppermute | solution.py:436
